TPU v7x, 32 devices: a whole 2x2x4 slice. The times are simulated.
32 devices in a mesh: lat: 4 (over y, x), lon: 8 (over z, core).
Axes of the slice: x: 2, y: 2, z: 4, core: 2. Of those that a mesh axis runs over, the one named last changes fastest.
Arguments:
- control: float32 [548, 32, 1024], P(None, 'lat', 'lon'), may hold values from -6 to 6
- std_dev: float32 [548], replicated, may hold values from 0.3 to 3
- col_dev: int32 [3072, 1], P(('lat', 'lon')), may hold values from 0 to 31; in each aligned block of 96 rows (0 to 95, 96 to 191, ...) at most 6 rows name the same one
- col_cell: int32 [3072], P(('lat', 'lon')), may hold values from 0 to 1023
- jacobian: bfloat16 [3072, 150, 548], P(('lat', 'lon')), may hold values from -0.25 to 0.25
- innovation: float32 [3072, 150], P(('lat', 'lon')), may hold values from -6 to 6
- inv_error: float32 [150], replicated, may hold values from 0.3 to 3
Outputs:
- departures: float32 [3072, 150], P(('lat', 'lon'))
- increment: float32 [548, 32, 1024], P(None, 'lat', 'lon')
- adjoint: float32 [548, 32, 1024], P(None, 'lat', 'lon')
Inputs may be any that keep to these rules, and one draw needn't show every extreme that they name: `col_dev`: among the soundings of one device (aligned blocks of 96 rows) at most 6 name the same device, and in every draw some device is named exactly 6 times by one block.
All inputs are finite; a program needn't handle non-finite values.
Results may differ from a plain program's by a relative error of at most 0.0025.
Values may be sent and summed in bfloat16 or wider, within the bound.
A program may use at most 128 MiB of HBM per device.

v0:
```python
import functools

import jax
import jax.numpy as jnp
from jax import lax
from jax.experimental import pallas as pl
from jax.experimental.pallas import tpu as pltpu
from jax.sharding import PartitionSpec as P

LHALF = 8
HIGHEST = lax.Precision.HIGHEST
MESH = pl.DeviceIdType.MESH


def tap_weights(offset, half_width):
    spread = 2.0 * half_width / 3.0
    taps = jnp.arange(-half_width, half_width + 1, dtype=jnp.int32).astype(jnp.float32)
    norm_total = jnp.sqrt(jnp.sum(jnp.exp(-taps * taps / (spread * spread))))
    weights = jnp.exp(-offset * offset / (2.0 * spread * spread)) / norm_total
    return jnp.where(jnp.abs(offset) <= half_width, weights, jnp.zeros_like(weights))


def band(out_count, in_count, half_width):
    row_index = jnp.arange(out_count, dtype=jnp.int32)[:, None]
    col_index = jnp.arange(in_count, dtype=jnp.int32)[None, :]
    return tap_weights((col_index - row_index - half_width).astype(jnp.float32), half_width)


def shifts(axis, wrap):
    peers = lax.axis_size(axis)
    up = [(i, (i + 1) % peers) for i in range(peers if wrap else peers - 1)]
    return up, [(j, i) for i, j in up]


def around(array, axis, wrap):
    up, down = shifts(axis, wrap)
    return lax.ppermute(array, axis, up), lax.ppermute(array, axis, down)


def halves(weights):
    high = weights.astype(jnp.bfloat16)
    return high, (weights - high.astype(jnp.float32)).astype(jnp.bfloat16)


def dot_split(data, weights):
    high, low = halves(weights)
    dot = lambda w: jnp.dot(data, w, preferred_element_type=jnp.float32)
    return dot(high) + dot(low)


def smooth(field, swapped, far):
    width, lat_rows, lon_cols = field.shape
    extended = jnp.concatenate([swapped.astype(jnp.float32), field, far.astype(jnp.float32)], axis=1)
    lat_band = band(lat_rows, lat_rows + 2 * LHALF, LHALF)
    before, middle, after = lat_band[:, :LHALF], lat_band[:, LHALF:-LHALF], lat_band[:, -LHALF:]
    odd = lax.axis_index("lat") % 2 == 1
    lat_band = jnp.concatenate([jnp.where(odd, before, after), middle, jnp.where(odd, after, before)], axis=1)
    field = jnp.einsum("ij,cjk->cik", lat_band, extended, precision=HIGHEST)
    lon_half, part = lon_cols // 2, width // 2
    rounded = field.astype(jnp.bfloat16)
    paired = lambda piece: jnp.concatenate([piece[:part], piece[part:]], axis=2)
    up, down = shifts("lon", True)
    left = lax.ppermute(paired(rounded[:, :, lon_half:]), "lon", up)
    right = lax.ppermute(paired(rounded[:, :, :lon_half]), "lon", down)
    lon_band = band(lon_cols, lon_cols + 2 * lon_half, lon_half).T
    edge = lambda w: jnp.concatenate(
        [jnp.concatenate([w, jnp.zeros_like(w)], 1), jnp.concatenate([jnp.zeros_like(w), w], 1)], 0
    )
    both = jnp.concatenate([left, right], axis=2).reshape(part * lat_rows, 2 * lon_cols)
    weights = jnp.concatenate([edge(lon_band[:lon_half]), edge(lon_band[-lon_half:])], 0)
    sides = dot_split(both, weights)
    sides = jnp.concatenate([sides[:, :lon_cols], sides[:, lon_cols:]], axis=0)
    own = jnp.dot(
        field.reshape(width * lat_rows, lon_cols), lon_band[lon_half:-lon_half], precision=HIGHEST
    )
    return (own + sides).reshape(width, lat_rows, lon_cols)


def exchange_kernel(
    lat, lon, cuts, tile_ref, wanted_ref, swap_ref, far_ref, requested_ref,
    swap_send, swap_recv, far_send, far_recv, want_send, want_recv,
):
    row, column = lax.axis_index("lat"), lax.axis_index("lon")
    devices, me = lat * lon, row * lon + column
    odd = row % 2
    partner, step = row + 1 - 2 * odd, 2 - 4 * odd
    onward = jnp.logical_and(row + step >= 0, row + step < lat)
    comes = jnp.logical_and(row - step >= 0, row - step < lat)
    place = lambda other: (other // lon, other % lon)

    barrier = pltpu.get_barrier_semaphore()

    def greet(d, carry):
        other = (me + d) % devices
        pl.semaphore_signal(barrier, inc=1, device_id=place(other), device_id_type=MESH)
        return carry

    lax.fori_loop(1, devices, greet, 0)
    pl.semaphore_wait(barrier, devices - 1)

    def request(dst, send, recv, other):
        return pltpu.make_async_remote_copy(
            src_ref=wanted_ref.at[0],
            dst_ref=requested_ref.at[dst],
            send_sem=want_send.at[send],
            recv_sem=want_recv.at[recv],
            device_id=place(other),
            device_id_type=MESH,
        )

    def ask(d, carry):
        other = (me + d) % devices
        request(me, other, me, other).start()
        return carry

    lax.fori_loop(1, devices, ask, 0)

    def swap(k):
        part = pl.ds(cuts[k], cuts[k + 1] - cuts[k])
        return pltpu.make_async_remote_copy(
            src_ref=tile_ref.at[part],
            dst_ref=swap_ref.at[part],
            send_sem=swap_send.at[k],
            recv_sem=swap_recv.at[k],
            device_id=(partner, column),
            device_id_type=MESH,
        )

    def forward(k):
        part = pl.ds(cuts[k], cuts[k + 1] - cuts[k])
        return pltpu.make_async_remote_copy(
            src_ref=swap_ref.at[part],
            dst_ref=far_ref.at[part],
            send_sem=far_send.at[k],
            recv_sem=far_recv.at[k],
            device_id=(row + step, column),
            device_id_type=MESH,
        )

    pieces = range(len(cuts) - 1)
    for k in pieces:
        swap(k).start()
    requested_ref[me] = wanted_ref[0]

    @pl.when(jnp.logical_not(comes))
    def _():
        far_ref[...] = jnp.zeros_like(far_ref)

    for k in pieces:
        swap(k).wait_recv()

        @pl.when(onward)
        def _():
            forward(k).start()

    def hear(d, carry):
        other = (me + d) % devices
        asked = request(other, other, other, other)
        asked.wait_send()
        asked.wait_recv()
        return carry

    lax.fori_loop(1, devices, hear, 0)
    for k in pieces:
        swap(k).wait_send()

        @pl.when(comes)
        def _():
            forward(k).wait_recv()

        @pl.when(onward)
        def _():
            forward(k).wait_send()


def exchange(tile, wanted):
    lat, lon = lax.axis_size("lat"), lax.axis_size("lon")
    devices, slots = lat * lon, wanted.shape[0]
    width, pieces = tile.shape[0], 6
    cuts = [width * k // pieces for k in range(pieces + 1)]
    wanted = jnp.pad(wanted, (0, -slots % 128))[None, None, :]
    vmem = pl.BlockSpec(memory_space=pltpu.VMEM)
    dma = pltpu.SemaphoreType.DMA
    swapped, far, requested = pl.pallas_call(
        functools.partial(exchange_kernel, lat, lon, cuts),
        in_specs=[vmem, vmem],
        out_specs=[vmem, vmem, vmem],
        out_shape=[
            jax.ShapeDtypeStruct(tile.shape, tile.dtype),
            jax.ShapeDtypeStruct(tile.shape, tile.dtype),
            jax.ShapeDtypeStruct((devices, *wanted.shape[1:]), wanted.dtype),
        ],
        scratch_shapes=[dma((pieces,))] * 4 + [dma((devices,))] * 2,
        compiler_params=pltpu.CompilerParams(collective_id=0, has_side_effects=True),
        name="exchange",
    )(tile, wanted)
    return swapped, far, requested[:, 0, :slots]


def lane_tiles(count):
    return -(-count // 128)


def sounding_kernel(channels, step, jac_ref, col_ref, innov_ref, inv_ref, dep_ref, out_ref, grad_ref):
    rows, width = col_ref.shape
    padded = dep_ref.shape[1]
    lanes = lax.broadcasted_iota(jnp.int32, (rows, padded), 1)
    columns = col_ref[...].astype(jnp.float32)
    dep_ref[...] = jnp.zeros_like(dep_ref)
    grad_ref[...] = jnp.zeros_like(grad_ref)

    def some(index, carry):
        weighted = []
        found = jnp.zeros(dep_ref.shape, jnp.float32)
        for k in range(step):
            channel = index * step + k
            product = jac_ref[channel].astype(jnp.float32) * columns
            observed = jnp.where(lanes == channel, innov_ref[...], 0.0)
            product = jnp.concatenate([product[:, :padded] - observed, product[:, padded:]], axis=1)
            departure = jnp.sum(product, axis=1, keepdims=True)
            found = found + jnp.where(lanes == channel, departure, 0.0)
            weight = (departure * inv_ref[0, channel]).astype(jnp.bfloat16)
            weighted.append(weight.astype(jnp.float32))
        dep_ref[...] += found
        total = grad_ref[...]
        for k in range(step):
            total = total + jac_ref[index * step + k].astype(jnp.float32) * weighted[k]
        grad_ref[...] = total
        return carry

    lax.fori_loop(0, channels // step, some, 0)
    out_ref[...] = jnp.zeros_like(out_ref)
    out_ref[:, :width] = grad_ref[...].astype(out_ref.dtype)


def sounding_step(jacobian, columns, innovation, inv_error):
    count, channels, width = jacobian.shape
    rows = 16
    step = next(n for n in (10, 8, 6, 5, 4, 3, 2, 1) if channels % n == 0)
    padded = lane_tiles(channels) * 128
    innovation = jnp.pad(innovation, ((0, 0), (0, padded - channels)))
    departures, grad = pl.pallas_call(
        functools.partial(sounding_kernel, channels, step),
        grid=(count // rows,),
        in_specs=[
            pl.BlockSpec((channels, rows, width), lambda i: (0, i, 0)),
            pl.BlockSpec((rows, width), lambda i: (i, 0)),
            pl.BlockSpec((rows, padded), lambda i: (i, 0)),
            pl.BlockSpec(memory_space=pltpu.SMEM),
        ],
        out_specs=[
            pl.BlockSpec((rows, padded), lambda i: (i, 0)),
            pl.BlockSpec((rows, lane_tiles(width) * 128), lambda i: (i, 0)),
        ],
        out_shape=[
            jax.ShapeDtypeStruct((count, padded), jnp.float32),
            jax.ShapeDtypeStruct((count, lane_tiles(width) * 128), jnp.bfloat16),
        ],
        scratch_shapes=[pltpu.VMEM((rows, width), jnp.float32)],
        name="soundings",
    )(jnp.transpose(jacobian, (1, 0, 2)), columns, innovation, inv_error[None, :])
    return departures[:, :channels], grad


def adjoint_kernel(near_ref, before_ref, after_ref, col_ref, row_ref, std_ref, out_ref):
    lon_cols = col_ref.shape[1]
    total = jnp.zeros((2 * lon_cols, near_ref.shape[1]), jnp.float32)
    for at, grads in enumerate((near_ref, before_ref, after_ref)):
        high, low = halves(col_ref[at] * row_ref[0, at])
        both = jnp.concatenate([high, low], axis=0)
        total = total + jnp.dot(both, grads[...], preferred_element_type=jnp.float32)
    total = (total[:lon_cols] + total[lon_cols:]) * std_ref[...]
    out_ref[...] = total.T[: out_ref.shape[0]]


def adjoint_step(grads, rows, columns_at, std_dev, lat_rows, lon_cols):
    slots, wide = grads[0].shape
    width = std_dev.shape[0]
    std_dev = jnp.pad(std_dev, (0, wide - width))
    down = jnp.arange(lat_rows)[:, None, None, None]
    row_weight = tap_weights((rows[None, :, None, :] - down).astype(jnp.float32), LHALF)
    along = jnp.arange(lon_cols)[None, :, None]
    col_weight = tap_weights((columns_at[:, None, :] - along).astype(jnp.float32), lon_cols // 2)
    whole = pl.BlockSpec((slots, wide), lambda i: (0, 0))
    return pl.pallas_call(
        adjoint_kernel,
        grid=(lat_rows,),
        in_specs=[
            whole,
            whole,
            whole,
            pl.BlockSpec((3, lon_cols, slots), lambda i: (0, 0, 0)),
            pl.BlockSpec((1, 3, 1, slots), lambda i: (i, 0, 0, 0)),
            pl.BlockSpec((1, wide), lambda i: (0, 0)),
        ],
        out_specs=pl.BlockSpec((width, lon_cols), lambda i: (0, i)),
        out_shape=jax.ShapeDtypeStruct((width, lat_rows * lon_cols), jnp.float32),
        name="adjoint",
    )(*grads, col_weight, row_weight, std_dev[None, :])


def local(control, std_dev, col_dev, col_cell, jacobian, innovation, inv_error):
    width, lat_rows, lon_cols = control.shape
    devices = lax.axis_size("lat") * lax.axis_size("lon")
    sound_count = col_cell.shape[0]
    slots_each = max(2, 2 * sound_count // devices)
    slots = devices * slots_each

    target = col_dev[:, 0]
    onehot = (target[:, None] == jnp.arange(devices, dtype=jnp.int32)[None, :]).astype(jnp.int32)
    below = jnp.arange(sound_count)[:, None] > jnp.arange(sound_count)[None, :]
    earlier = jnp.dot(
        below.astype(jnp.bfloat16), onehot.astype(jnp.bfloat16), preferred_element_type=jnp.float32
    ).astype(jnp.int32)
    order_in = jnp.sum(earlier * onehot, axis=1)
    slot = target * slots_each + order_in
    wanted = jnp.zeros((slots,), jnp.int32).at[slot].set(col_cell)
    swapped, far, table = exchange(control.astype(jnp.bfloat16), wanted)
    lat_at, lon_at = lax.axis_index("lat"), lax.axis_index("lon")
    lat_devices, lon_devices = lax.axis_size("lat"), lax.axis_size("lon")

    def asked_of(lat_shift, lon_shift):
        row = jnp.clip(lat_at + lat_shift, 0, lat_devices - 1)
        owner = row * lon_devices + (lon_at + lon_shift) % lon_devices
        return lax.dynamic_slice(table, (0, owner * slots_each), (devices, slots_each))

    requested = asked_of(0, 0).reshape(-1)

    increment = smooth(control, swapped, far) * std_dev[:, None, None]
    flat_field = increment.reshape(width, lat_rows * lon_cols)
    picked = jnp.take(flat_field, requested, axis=1).T.astype(jnp.bfloat16)
    returned = lax.all_to_all(
        picked.reshape(devices, slots_each, width), ("lat", "lon"), split_axis=0, concat_axis=0, tiled=True
    )
    columns = returned.reshape(slots, width)[slot]
    departures, column_grad = sounding_step(jacobian, columns, innovation, inv_error)
    wide = column_grad.shape[1]
    outgoing = jnp.zeros((slots, wide), jnp.bfloat16).at[slot].set(column_grad)
    arrived = lax.all_to_all(
        outgoing.reshape(devices, slots_each, wide), ("lat", "lon"), split_axis=0, concat_axis=0, tiled=True
    ).reshape(slots, wide)
    near = jnp.concatenate([arrived, *around(arrived, "lat", False)], axis=0)
    grads = (near, *around(near, "lon", True))
    order = (0, -1, 1)
    cells = jnp.stack([jnp.stack([asked_of(up, along) for up in order]) for along in order])
    cells = cells.reshape(3, 3, slots)
    shift = jnp.array(order, jnp.int32)
    rows = (cells // lon_cols + lat_rows * shift[None, :, None]).reshape(3, 3 * slots)
    columns_at = (cells % lon_cols + lon_cols * shift[:, None, None]).reshape(3, 3 * slots)
    adjoint = adjoint_step(grads, rows, columns_at, std_dev, lat_rows, lon_cols)
    return (departures, increment, adjoint.reshape(width, lat_rows, lon_cols))


def solution(mesh):
    placed = (
        P(None, "lat", "lon"),
        P(),
        P(("lat", "lon"), None),
        P(("lat", "lon")),
        P(("lat", "lon"), None, None),
        P(("lat", "lon"), None),
        P(),
    )
    return jax.shard_map(
        local,
        mesh=mesh,
        in_specs=placed,
        out_specs=(P(("lat", "lon"), None), P(None, "lat", "lon"), P(None, "lat", "lon")),
        check_vma=False,
    )
```

profile of v0, /device:TPU:2, one launch (start us, length us, event | category | flops | bytes accessed | tf_op | source)
XLA Modules:
  0.0 185.6 jit_solution(815949851321321149)
XLA Ops:
  0.6 0.6 fusion.44
  2.0 2.7 %convert_element_type.74.tile_ref = bf16[548,8,128]{2,1,0:T(8,128)(2,1)} convert(f32[548,8,128]{2,1,0:T(8,128)} %param.8) | non-fusion elementwise | flops 561152 | bytes 3366912 | tf_op jit(solution)/shard_map/convert_element_type | solution.py:318
  4.7 0.2 fusion.8
  4.9 1.0 scatter_custom_fusion
  5.9 0.6 pad.16
  6.5 40.1 %exchange.1 = (bf16[548,8,128]{2,1,0:T(8,128)(2,1)}, bf16[548,8,128]{2,1,0:T(8,128)(2,1)}, s32[32,1,256]{2,1,0:T(1,128)}) custom-call(bf16[548,8,128]{2,1,0:T(8,128)(2,1)} %convert_element_type.74.tile_ref, s32[1,1,256]{2,1,0:T(1,128)} %bitcast.60), custom_call_target="tpu_custom_call" | custom-call | tf_op jit(solution)/shard_map/exchange/pallas_call | solution.py:184
  46.6 1.5 convert_element_type.79
  48.2 0.1 convert_element_type.78
  48.4 1.4 copy-done
  49.8 3.5 %bitcast_convert_fusion = (bf16[548,8,128]{2,1,0:T(8,128)(2,1)S(1)}, f32[548,128,8]{1,2,0:T(8,128)S(1)}) fusion(f32[8,8]{1,0:T(8,128)S(1)} %get-tuple-element.55, f32[8,8]{1,0:T(8,128)S(1)} %get-tuple-element.54, f32[8,8]{1,0:T(8,128)S(1)} %get-tuple-element.53, f32[548,8,128]{2,1,0:T(8,128)S(1)} %convert_element_type.79, f32[548,8,128]{2,1,0:T(8,128)S(1)} %copy-done, ...), kind=kOutput, calls=%fused_computation.14 | convolution fusion | flops 165540224 | bytes 10101504 | tf_op jit(solution)/shard_map/ij,cjk->cik/dot_general | solution.py:58
  53.3 0.4 fusion.59
  53.8 0.3 pad_maximum_fusion.1
  54.1 0.3 pad_maximum_fusion
  54.5 0.5 collective-permute-start
  55.0 0.6 fusion.41
  56.4 0.5 broadcast.319
  57.0 2.3 %constant_dynamic-slice_fusion.7 = (s32[32,1,6]{2,1,0:T(1,128)}, s32[32,1,6]{2,1,0:T(1,128)}, s32[32,1,6]{2,1,0:T(1,128)}, s32[32,1,6]{2,1,0:T(1,128)}, s32[32,1...) fusion(s32[32,1,192]{2,1,0:T(1,128)S(1)} %bitcast.48, ...), kind=kLoop, calls=%fused_computation.102 | loop fusion | bytes 14632 | tf_op jit(solution)/shard_map/dynamic_slice | solution.py:325
  59.2 0.1 reshape.335
  59.4 0.8 reshape.331
  60.2 6.5 %collective-permute-done.1 = bf16[274,8,128]{2,1,0:T(8,128)(2,1)} collective-permute-done((bf16[274,8,128]{2,1,0:T(8,128)(2,1)S(1)}, bf16[274,8,128]{2,1,0:T(8,128)(2,1)}, u32[]{:S(2)}, u32[]{:S(2)}) %collective-permute-start.1) | collective-permute-done | bytes 561184 | tf_op jit(solution)/shard_map/ppermute | solution.py:64
  66.7 1.9 %collective-permute-done = bf16[274,8,128]{2,1,0:T(8,128)(2,1)} collective-permute-done((bf16[274,8,128]{2,1,0:T(8,128)(2,1)S(1)}, bf16[274,8,128]{2,1,0:T(8,128)(2,1)}, u32[]{:S(2)}, u32[]{:S(2)}) %collective-permute-start) | collective-permute-done | bytes 561184 | tf_op jit(solution)/shard_map/ppermute | solution.py:63
  68.6 1.7 fusion.13
  70.3 1.7 convolution_add_fusion.1
  72.0 0.1 fusion.58
  72.1 0.5 copy-done.16
  72.7 5.5 %bitcast_multiply_fusion = (f32[548,8,128]{2,1,0:T(8,128)}, f32[4384,128]{1,0:T(8,128)}) fusion(f32[548]{0:T(1024)S(1)} %copy-done.16, f32[2192,128]{1,0:T(8,128)S(1)} %get-tuple-element.34, f32[2192,128]{1,0:T(8,128)S(1)} %get-tuple-element.33, f32[256,128]{1,0:T(8,128)S(1)} %fusion.19, f32[548,128,8]{1,2,0:T(8,128)S(1)} %get-tuple-element.57), kind=kOutput, calls=%fused_computation.13 | convolution fusion | flops 863612928 | bytes 9048064 | tf_op jit(solution)/shard_map/dot_general | solution.py:73
  78.1 2.4 %reshape.334 = f32[548,1024]{1,0:T(8,128)S(1)} reshape(f32[4384,128]{1,0:T(8,128)} %get-tuple-element.59) | data formatting | bytes 4489216 | tf_op jit(solution)/shard_map/reshape | solution.py:76
  80.5 0.2 broadcast_multiply_fusion
  80.7 0.7 copy.62
  81.5 1.0 gather_fusion
  82.5 0.1 select_convert_fusion
  82.6 0.8 reshape.336
  83.5 3.5 %all-to-all-start = ((bf16[32,6,548]{2,1,0:T(8,128)(2,1)}), bf16[32,6,548]{2,1,0:T(8,128)(2,1)S(1)}, u32[]{:S(2)}, u32[]{:S(2)}) async-start(bf16[32,6,548]{2,1,0:T(8,128)(2,1)} %reshape.336), calls=%async_computation | async-start | bytes 655360 | tf_op jit(solution)/shard_map/all_to_all | solution.py:332
  87.0 0.1 copy.63
  87.1 0.6 pad.17.innov_ref
  87.7 9.3 %all-to-all-done = bf16[32,6,548]{2,1,0:T(8,128)(2,1)S(1)} async-done(((bf16[32,6,548]{2,1,0:T(8,128)(2,1)}), bf16[32,6,548]{2,1,0:T(8,128)(2,1)S(1)}, u32[]{:S(2)}, u32[]{:S(2)}) %all-to-all-start) | async-done | bytes 210464 | tf_op jit(solution)/shard_map/all_to_all | solution.py:332
  97.0 0.1 reshape.337
  97.2 1.4 gather_fusion.1
  98.6 16.7 %soundings.1 = (f32[96,256]{1,0:T(8,128)}, bf16[96,640]{1,0:T(8,128)(2,1)}) custom-call(bf16[150,96,548]{2,1,0:T(8,128)(2,1)} %bitcast.45, bf16[96,548]{1,0:T(8,128)(2,1)} %gather_fusion.1, f32[96,256]{1,0:T(8,128)} %pad.17.innov_ref, f32[1,150]{1,0:T(1,128)} %bitcast.62), custom_call_target="tpu_custom_call" | custom-call | tf_op jit(solution)/shard_map/soundings/pallas_call | solution.py:242
  115.3 1.4 scatter_custom_fusion.1
  116.7 0.8 reshape.339
  117.5 4.6 %all-to-all-start.1 = ((bf16[32,6,640]{2,1,0:T(8,128)(2,1)}), bf16[32,6,640]{2,1,0:T(8,128)(2,1)S(1)}, u32[]{:S(2)}, u32[]{:S(2)}) async-start(bf16[32,6,640]{2,1,0:T(8,128)(2,1)} %reshape.339), calls=%async_computation.1 | async-start | bytes 655360 | tf_op jit(solution)/shard_map/all_to_all | solution.py:339
  122.4 9.9 %all-to-all-done.1 = bf16[32,6,640]{2,1,0:T(8,128)(2,1)S(1)} async-done(((bf16[32,6,640]{2,1,0:T(8,128)(2,1)}), bf16[32,6,640]{2,1,0:T(8,128)(2,1)S(1)}, u32[]{:S(2)}, u32[]{:S(2)}) %all-to-all-start.1) | async-done | bytes 245792 | tf_op jit(solution)/shard_map/all_to_all | solution.py:339
  132.4 4.1 %collective-permute-start.2 = (bf16[192,640]{1,0:T(8,128)(2,1)S(1)}, bf16[192,640]{1,0:T(8,128)(2,1)S(1)}, u32[]{:S(2)}, u32[]{:S(2)}) collective-permute-start(bf16[192,640]{1,0:T(8,128)(2,1)S(1)} %reshape.340), channel_id=1, source_target_pairs={{0,8},{8,16},{16,24},{1,9},{9,17},{17,25},{2,10},{10,18},{18,26},{... | collective-permute-start | bytes 737288 | tf_op jit(solution)/shard_map/ppermute | solution.py:37
  136.8 1.9 %collective-permute-start.3 = (bf16[192,640]{1,0:T(8,128)(2,1)S(1)}, bf16[192,640]{1,0:T(8,128)(2,1)S(1)}, u32[]{:S(2)}, u32[]{:S(2)}) collective-permute-start(bf16[192,640]{1,0:T(8,128)(2,1)S(1)} %reshape.340), channel_id=1, source_target_pairs={{8,0},{16,8},{24,16},{9,1},{17,9},{25,17},{10,2},{18,10},{26,18},{... | collective-permute-start | bytes 737288 | tf_op jit(solution)/shard_map/ppermute | solution.py:37
  139.0 3.9 %collective-permute-done.2 = bf16[192,640]{1,0:T(8,128)(2,1)S(1)} collective-permute-done((bf16[192,640]{1,0:T(8,128)(2,1)S(1)}, bf16[192,640]{1,0:T(8,128)(2,1)S(1)}, u32[]{:S(2)}, u32[]{:S(2)}) %collective-permute-start.2) | collective-permute-done | bytes 245792 | tf_op jit(solution)/shard_map/ppermute | solution.py:37
  142.9 5.6 %collective-permute-done.3 = bf16[192,640]{1,0:T(8,128)(2,1)S(1)} collective-permute-done((bf16[192,640]{1,0:T(8,128)(2,1)S(1)}, bf16[192,640]{1,0:T(8,128)(2,1)S(1)}, u32[]{:S(2)}, u32[]{:S(2)}) %collective-permute-start.3) | collective-permute-done | bytes 245792 | tf_op jit(solution)/shard_map/ppermute | solution.py:37
  148.7 3.5 %collective-permute-start.5 = (bf16[576,640]{1,0:T(8,128)(2,1)S(1)}, bf16[576,640]{1,0:T(8,128)(2,1)S(1)}, u32[]{:S(2)}, u32[]{:S(2)}) collective-permute-start(bf16[576,640]{1,0:T(8,128)(2,1)S(1)} %constant_dynamic-update-slice_fusion.near_ref), channel_id=1, source_target_pairs={{1,0},{2,1},{3,2},{4,3},{5,4},{6,5},{7,6},{0,7},{9,8},{10,9},{11,1... | collective-permute-start | bytes 2211848 | tf_op jit(solution)/shard_map/ppermute | solution.py:37
  152.2 0.1 copy.75
  152.3 0.1 stack.62
  152.5 0.1 copy.71
  152.6 0.1 stack.57
  152.7 0.1 copy.67
  152.8 0.1 stack.52
  153.1 0.6 broadcast_in_dim.65.std_ref
  153.8 0.8 compare_select_fusion.row_ref
  154.6 1.3 fusion.12.col_ref
  155.9 0.7 copy.76
  156.6 12.3 %collective-permute-done.4.before_ref = bf16[576,640]{1,0:T(8,128)(2,1)S(1)} collective-permute-done((bf16[576,640]{1,0:T(8,128)(2,1)S(1)}, bf16[576,640]{1,0:T(8,128)(2,1)S(1)}, u32[]{:S(2)}, u32[]{:S(2)}) %collective-permute-start.4) | collective-permute-done | bytes 737312 | tf_op jit(solution)/shard_map/ppermute | solution.py:37
  168.9 0.9 copy-done.3
  169.8 0.9 copy-done.4
  170.7 11.3 %adjoint.1 = f32[548,1024]{1,0:T(8,128)} custom-call(bf16[576,640]{1,0:T(8,128)(2,1)} %copy-done.1, bf16[576,640]{1,0:T(8,128)(2,1)} %copy-done.3, bf16[576,640]{1,0:T(8,128)(2,1)} %copy-done.4, f32[3,128,576]{2,1,0:T(8,128)} %fusion.12.col_ref, f32[8,3,1,576]{3,2,1,0:T(1,128)} %compare_select_fusion.row_ref, f32[1,640]{1,0:T(1,128)} %broadcast_in_dim.65.std_ref), custom_call_target="tpu_custom_call" | custom-call | tf_op jit(solution)/shard_map/adjoint/pallas_call | solution.py:285
  181.9 2.1 %copy.77 = f32[69,8,8,128]{3,2,1,0:T(8,128)S(1)} copy(f32[69,8,8,128]{3,1,2,0:T(8,128)} %bitcast.46) | data formatting | bytes 4521984
  184.1 1.5 slice.75
  (72 shorter events, 1.6 us)
Async XLA Ops:
  0.6 4.1 %copy-start.21 = (s32[96,1]{0,1:T(1,128)S(1)}, s32[96,1]{0,1:T(1,128)}, u32[]{:S(2)}) copy-start(s32[96,1]{0,1:T(1,128)} %param.10) | copy-start | bytes 1156
  4.9 43.2 %copy-start.19 = (s32[96]{0:T(128)}, s32[96]{0:T(128)S(1)}, u32[]{:S(2)}) copy-start(s32[96]{0:T(128)S(1)} %fusion.45) | copy-start | bytes 1156
  46.6 1.6 copy-start.2
  48.1 1.7 copy-start
  53.7 3.2 %copy-start.5 = (s32[32,1,256]{2,1,0:T(1,128)S(1)}, s32[32,1,256]{2,1,0:T(1,128)}, u32[]{:S(2)}) copy-start(s32[32,1,256]{2,1,0:T(1,128)} %get-tuple-element.8) | copy-start | bytes 98308
  54.1 12.6 %collective-permute-start.1 = (bf16[274,8,128]{2,1,0:T(8,128)(2,1)S(1)}, bf16[274,8,128]{2,1,0:T(8,128)(2,1)}, u32[]{:S(2)}, u32[]{:S(2)}) collective-permute-start(bf16[274,8,128]{2,1,0:T(8,128)(2,1)S(1)} %pad_maximum_fusion.1), channel_id=1, source_target_pairs={{1,0},{2,1},{3,2},{4,3},{5,4},{6,5},{7,6},{0,7},{9,8},{10,9},{11,1... | collective-permute-start | bytes 1683464 | tf_op jit(solution)/shard_map/ppermute | solution.py:64
  54.5 14.1 %collective-permute-start = (bf16[274,8,128]{2,1,0:T(8,128)(2,1)S(1)}, bf16[274,8,128]{2,1,0:T(8,128)(2,1)}, u32[]{:S(2)}, u32[]{:S(2)}) collective-permute-start(bf16[274,8,128]{2,1,0:T(8,128)(2,1)S(1)} %pad_maximum_fusion), channel_id=1, source_target_pairs={{0,1},{1,2},{2,3},{3,4},{4,5},{5,6},{6,7},{7,0},{8,9},{9,10},{10,1... | collective-permute-start | bytes 1683464 | tf_op jit(solution)/shard_map/ppermute | solution.py:63
  72.0 0.7 copy-start.16
  81.5 5.5 %copy-start.7 = (f32[96,150]{0,1:T(8,128)S(1)}, f32[96,150]{0,1:T(8,128)}, u32[]{:S(2)}) copy-start(f32[96,150]{0,1:T(8,128)} %param.13) | copy-start | bytes 172804
  81.5 6.2 %copy-start.20 = (s32[96]{0:T(128)S(1)}, s32[96]{0:T(128)}, u32[]{:S(2)}) copy-start(s32[96]{0:T(128)} %copy-done.19) | copy-start | bytes 1156
  83.5 13.5 %all-to-all-start = ((bf16[32,6,548]{2,1,0:T(8,128)(2,1)}), bf16[32,6,548]{2,1,0:T(8,128)(2,1)S(1)}, u32[]{:S(2)}, u32[]{:S(2)}) async-start(bf16[32,6,548]{2,1,0:T(8,128)(2,1)} %reshape.336), calls=%async_computation | async-start | bytes 655360 | tf_op jit(solution)/shard_map/all_to_all | solution.py:332
  98.6 23.5 %copy-start.15 = (s32[32,1,6]{2,1,0:T(1,128)S(1)}, s32[32,1,6]{2,1,0:T(1,128)}, u32[]{:S(2)}) copy-start(s32[32,1,6]{2,1,0:T(1,128)} %get-tuple-element.42) | copy-start | bytes 2308
  98.6 23.6 %copy-start.14 = (s32[32,1,6]{2,1,0:T(1,128)S(1)}, s32[32,1,6]{2,1,0:T(1,128)}, u32[]{:S(2)}) copy-start(s32[32,1,6]{2,1,0:T(1,128)} %get-tuple-element.43) | copy-start | bytes 2308
  98.6 23.7 %copy-start.13 = (s32[32,1,6]{2,1,0:T(1,128)S(1)}, s32[32,1,6]{2,1,0:T(1,128)}, u32[]{:S(2)}) copy-start(s32[32,1,6]{2,1,0:T(1,128)} %get-tuple-element.44) | copy-start | bytes 2308
  98.6 37.9 %copy-start.12 = (s32[32,1,6]{2,1,0:T(1,128)S(1)}, s32[32,1,6]{2,1,0:T(1,128)}, u32[]{:S(2)}) copy-start(s32[32,1,6]{2,1,0:T(1,128)} %get-tuple-element.45) | copy-start | bytes 2308
  98.6 38.0 %copy-start.11 = (s32[32,1,6]{2,1,0:T(1,128)S(1)}, s32[32,1,6]{2,1,0:T(1,128)}, u32[]{:S(2)}) copy-start(s32[32,1,6]{2,1,0:T(1,128)} %get-tuple-element.46) | copy-start | bytes 2308
  98.6 38.1 %copy-start.10 = (s32[32,1,6]{2,1,0:T(1,128)S(1)}, s32[32,1,6]{2,1,0:T(1,128)}, u32[]{:S(2)}) copy-start(s32[32,1,6]{2,1,0:T(1,128)} %get-tuple-element.47) | copy-start | bytes 2308
  115.3 23.5 %copy-start.9 = (s32[32,1,6]{2,1,0:T(1,128)S(1)}, s32[32,1,6]{2,1,0:T(1,128)}, u32[]{:S(2)}) copy-start(s32[32,1,6]{2,1,0:T(1,128)} %get-tuple-element.48) | copy-start | bytes 2308
  115.3 23.6 %copy-start.8 = (s32[32,1,6]{2,1,0:T(1,128)S(1)}, s32[32,1,6]{2,1,0:T(1,128)}, u32[]{:S(2)}) copy-start(s32[32,1,6]{2,1,0:T(1,128)} %get-tuple-element.41) | copy-start | bytes 2308
  115.3 37.7 %copy-start.18 = (s32[3]{0:T(128)S(1)}, s32[3]{0:T(128)}, u32[]{:S(2)}) copy-start(s32[3]{0:T(128)} %constant.176) | copy-start | bytes 40
  115.3 38.4 %copy-start.17 = (s32[3]{0:T(128)S(1)}, s32[3]{0:T(128)}, u32[]{:S(2)}) copy-start(s32[3]{0:T(128)} %constant.175) | copy-start | bytes 40
  117.5 38.3 %copy-start.6 = (f32[96,256]{1,0:T(8,128)S(1)}, f32[96,256]{1,0:T(8,128)}, u32[]{:S(2)}) copy-start(f32[96,256]{1,0:T(8,128)} %get-tuple-element.11) | copy-start | bytes 294916
  117.5 14.8 %all-to-all-start.1 = ((bf16[32,6,640]{2,1,0:T(8,128)(2,1)}), bf16[32,6,640]{2,1,0:T(8,128)(2,1)S(1)}, u32[]{:S(2)}, u32[]{:S(2)}) async-start(bf16[32,6,640]{2,1,0:T(8,128)(2,1)} %reshape.339), calls=%async_computation.1 | async-start | bytes 655360 | tf_op jit(solution)/shard_map/all_to_all | solution.py:339
  132.4 10.5 %collective-permute-start.2 = (bf16[192,640]{1,0:T(8,128)(2,1)S(1)}, bf16[192,640]{1,0:T(8,128)(2,1)S(1)}, u32[]{:S(2)}, u32[]{:S(2)}) collective-permute-start(bf16[192,640]{1,0:T(8,128)(2,1)S(1)} %reshape.340), channel_id=1, source_target_pairs={{0,8},{8,16},{16,24},{1,9},{9,17},{17,25},{2,10},{10,18},{18,26},{... | collective-permute-start | bytes 737288 | tf_op jit(solution)/shard_map/ppermute | solution.py:37
  136.8 11.8 %collective-permute-start.3 = (bf16[192,640]{1,0:T(8,128)(2,1)S(1)}, bf16[192,640]{1,0:T(8,128)(2,1)S(1)}, u32[]{:S(2)}, u32[]{:S(2)}) collective-permute-start(bf16[192,640]{1,0:T(8,128)(2,1)S(1)} %reshape.340), channel_id=1, source_target_pairs={{8,0},{16,8},{24,16},{9,1},{17,9},{25,17},{10,2},{18,10},{26,18},{... | collective-permute-start | bytes 737288 | tf_op jit(solution)/shard_map/ppermute | solution.py:37
  148.6 20.4 %copy-start.1 = (bf16[576,640]{1,0:T(8,128)(2,1)}, bf16[576,640]{1,0:T(8,128)(2,1)S(1)}, u32[]{:S(2)}) copy-start(bf16[576,640]{1,0:T(8,128)(2,1)S(1)} %constant_dynamic-update-slice_fusion.near_ref) | copy-start | bytes 2211844
  148.6 20.3 %collective-permute-start.4 = (bf16[576,640]{1,0:T(8,128)(2,1)S(1)}, bf16[576,640]{1,0:T(8,128)(2,1)S(1)}, u32[]{:S(2)}, u32[]{:S(2)}) collective-permute-start(bf16[576,640]{1,0:T(8,128)(2,1)S(1)} %constant_dynamic-update-slice_fusion.near_ref), channel_id=1, source_target_pairs={{0,1},{1,2},{2,3},{3,4},{4,5},{5,6},{6,7},{7,0},{8,9},{9,10},{10,1... | collective-permute-start | bytes 2211848 | tf_op jit(solution)/shard_map/ppermute | solution.py:37
  148.7 20.3 %collective-permute-start.5 = (bf16[576,640]{1,0:T(8,128)(2,1)S(1)}, bf16[576,640]{1,0:T(8,128)(2,1)S(1)}, u32[]{:S(2)}, u32[]{:S(2)}) collective-permute-start(bf16[576,640]{1,0:T(8,128)(2,1)S(1)} %constant_dynamic-update-slice_fusion.near_ref), channel_id=1, source_target_pairs={{1,0},{2,1},{3,2},{4,3},{5,4},{6,5},{7,6},{0,7},{9,8},{10,9},{11,1... | collective-permute-start | bytes 2211848 | tf_op jit(solution)/shard_map/ppermute | solution.py:37
  168.9 0.9 copy-start.3
  169.8 0.9 copy-start.4
where the time goes:
time: 188 us; the launch traced here: 186 us
  Pallas kernels  68.1 us (36%)
  waiting for transfers between devices  49.4 us (26%)
  local copies, waits for them, and re-layouts  25.8 us (14%)
  starting transfers between devices  18.3 us (10%)
  matrix products  12.5 us (7%)
  other arithmetic  8.94 us (5%)
  between operations  2.54 us (1%)
    pallas_call x1, Pallas kernels, exchange(): pl.pallas_call(functools.partial(exchange_kernel, lat, lon, cuts), in_spe...  40.1 us
    ppermute x4, waiting for transfers between devices, around(): return (lax.ppermute(array, axis, up), lax.ppermute(array, axis, down))  21.8 us
    pallas_call x1, Pallas kernels, sounding_step(): pl.pallas_call(functools.partial(sounding_kernel, channels, step), grid=(...  16.7 us
    pallas_call x1, Pallas kernels, adjoint_step(): pl.pallas_call(adjoint_kernel, grid=(lat_rows,), in_specs=[whole, whole,...  11.3 us
    all_to_all x1, waiting for transfers between devices, local(): lax.all_to_all(outgoing.reshape(devices, slots_each, wide), ('lat', 'lon'...  9.92 us
    ppermute x4, starting transfers between devices, around(): return (lax.ppermute(array, axis, up), lax.ppermute(array, axis, down))  9.63 us
    all_to_all x1, waiting for transfers between devices, local(): lax.all_to_all(picked.reshape(devices, slots_each, width), ('lat', 'lon')...  9.28 us
    unnamed x49, local copies, waits for them, and re-layouts  6.79 us
  transfers between devices with their start and end apart: 8, of which 7 were waited for; matrix products, arithmetic and copies ran while one was open for 6% of the time, Pallas kernels for 0%

commit v1 on v0

--- a/solution.py
+++ b/solution.py
@@ -1,4 +1,5 @@
 import functools
+import math
 
 import jax
 import jax.numpy as jnp
@@ -20,12 +21,6 @@
     return jnp.where(jnp.abs(offset) <= half_width, weights, jnp.zeros_like(weights))
 
 
-def band(out_count, in_count, half_width):
-    row_index = jnp.arange(out_count, dtype=jnp.int32)[:, None]
-    col_index = jnp.arange(in_count, dtype=jnp.int32)[None, :]
-    return tap_weights((col_index - row_index - half_width).astype(jnp.float32), half_width)
-
-
 def shifts(axis, wrap):
     peers = lax.axis_size(axis)
     up = [(i, (i + 1) % peers) for i in range(peers if wrap else peers - 1)]
@@ -42,44 +37,39 @@
     return high, (weights - high.astype(jnp.float32)).astype(jnp.bfloat16)
 
 
-def dot_split(data, weights):
-    high, low = halves(weights)
-    dot = lambda w: jnp.dot(data, w, preferred_element_type=jnp.float32)
-    return dot(high) + dot(low)
-
-
-def smooth(field, swapped, far):
-    width, lat_rows, lon_cols = field.shape
-    extended = jnp.concatenate([swapped.astype(jnp.float32), field, far.astype(jnp.float32)], axis=1)
-    lat_band = band(lat_rows, lat_rows + 2 * LHALF, LHALF)
-    before, middle, after = lat_band[:, :LHALF], lat_band[:, LHALF:-LHALF], lat_band[:, -LHALF:]
-    odd = lax.axis_index("lat") % 2 == 1
-    lat_band = jnp.concatenate([jnp.where(odd, before, after), middle, jnp.where(odd, after, before)], axis=1)
-    field = jnp.einsum("ij,cjk->cik", lat_band, extended, precision=HIGHEST)
-    lon_half, part = lon_cols // 2, width // 2
-    rounded = field.astype(jnp.bfloat16)
-    paired = lambda piece: jnp.concatenate([piece[:part], piece[part:]], axis=2)
-    up, down = shifts("lon", True)
-    left = lax.ppermute(paired(rounded[:, :, lon_half:]), "lon", up)
-    right = lax.ppermute(paired(rounded[:, :, :lon_half]), "lon", down)
-    lon_band = band(lon_cols, lon_cols + 2 * lon_half, lon_half).T
-    edge = lambda w: jnp.concatenate(
-        [jnp.concatenate([w, jnp.zeros_like(w)], 1), jnp.concatenate([jnp.zeros_like(w), w], 1)], 0
-    )
-    both = jnp.concatenate([left, right], axis=2).reshape(part * lat_rows, 2 * lon_cols)
-    weights = jnp.concatenate([edge(lon_band[:lon_half]), edge(lon_band[-lon_half:])], 0)
-    sides = dot_split(both, weights)
-    sides = jnp.concatenate([sides[:, :lon_cols], sides[:, lon_cols:]], axis=0)
-    own = jnp.dot(
-        field.reshape(width * lat_rows, lon_cols), lon_band[lon_half:-lon_half], precision=HIGHEST
-    )
-    return (own + sides).reshape(width, lat_rows, lon_cols)
-
-
-def exchange_kernel(
-    lat, lon, cuts, tile_ref, wanted_ref, swap_ref, far_ref, requested_ref,
-    swap_send, swap_recv, far_send, far_recv, want_send, want_recv,
+def tap_value(offset, half_width):
+    spread = 2.0 * half_width / 3.0
+    norm_total = math.sqrt(sum(math.exp(-e * e / (spread * spread)) for e in range(-half_width, half_width + 1)))
+    weights = jnp.exp(-offset * offset / (2.0 * spread * spread)) / norm_total
+    return jnp.where(jnp.abs(offset) <= half_width, weights, 0.0)
+
+
+GROUP = 256
+CHUNK = 2 * GROUP
+
+
+def matmul(left, right):
+    return jnp.dot(left, right, preferred_element_type=jnp.float32)
+
+
+def across(left, right):
+    return lax.dot_general(left, right, (((1,), (1,)), ((), ())), preferred_element_type=jnp.float32)
+
+
+def dense_kernel(
+    lat, lon, lat_rows, slots_each,
+    ctrl_ref, wanted_ref, std_ref,
+    inc_ref, table_ref, got_ref,
+    own_ref, swap_ref, far_ref, g_ref, to_right_ref, to_left_ref, from_left_ref, from_right_ref,
+    band_ref, mid_ref, edge_ref, std_row_ref, cell_ref, row_ref, pick_ref,
+    swap_send, swap_recv, far_send, far_recv, lon_send, lon_recv,
+    want_send, want_recv, col_send, col_recv,
 ):
+    rows, lon_cols = ctrl_ref.shape
+    width = rows // lat_rows
+    full, rest = rows // CHUNK, rows % CHUNK
+    log_lat, log_lon = lat_rows.bit_length() - 1, lon_cols.bit_length() - 1
+    lon_half = lon_cols // 2
     row, column = lax.axis_index("lat"), lax.axis_index("lon")
     devices, me = lat * lon, row * lon + column
     odd = row % 2
@@ -87,71 +77,117 @@
     onward = jnp.logical_and(row + step >= 0, row + step < lat)
     comes = jnp.logical_and(row - step >= 0, row - step < lat)
     place = lambda other: (other // lon, other % lon)
+    iota = lambda shape, axis: lax.broadcasted_iota(jnp.int32, shape, axis)
 
     barrier = pltpu.get_barrier_semaphore()
 
     def greet(d, carry):
-        other = (me + d) % devices
-        pl.semaphore_signal(barrier, inc=1, device_id=place(other), device_id_type=MESH)
+        pl.semaphore_signal(barrier, inc=1, device_id=place((me + d) % devices), device_id_type=MESH)
         return carry
 
     lax.fori_loop(1, devices, greet, 0)
+
+    def chunk_of(k):
+        return pl.ds(pl.multiple_of(k * CHUNK, CHUNK), CHUNK)
+
+    def half_of(k):
+        return pl.ds(pl.multiple_of(k * GROUP, GROUP), GROUP)
+
+    last, last_half = pl.ds(full * CHUNK, rest), pl.ds(full * GROUP, rest // 2)
+
+    def remote(source, target, send, recv, device):
+        return pltpu.make_async_remote_copy(
+            src_ref=source, dst_ref=target, send_sem=send, recv_sem=recv, device_id=device, device_id_type=MESH
+        )
+
+    def request(dst, send, recv, other):
+        return remote(wanted_ref.at[0], table_ref.at[dst], want_send.at[send], want_recv.at[recv], place(other))
+
+    def swap(k, part):
+        return remote(own_ref.at[part], swap_ref.at[part], swap_send.at[k], swap_recv.at[k], (partner, column))
+
+    def forward(k, part):
+        return remote(swap_ref.at[part], far_ref.at[part], far_send.at[k], far_recv.at[k], (row + step, column))
+
+    def to_right(k, part):
+        return remote(
+            to_right_ref.at[part], from_left_ref.at[part], lon_send.at[0, k], lon_recv.at[0, k],
+            (row, (column + 1) % lon),
+        )
+
+    def to_left(k, part):
+        return remote(
+            to_left_ref.at[part], from_right_ref.at[part], lon_send.at[1, k], lon_recv.at[1, k],
+            (row, (column + lon - 1) % lon),
+        )
+
+    def back(d, group):
+        part = pl.ds(pl.multiple_of(group * lon_cols, lon_cols), lon_cols)
+        return remote(
+            pick_ref.at[d, :, part], got_ref.at[me, :, part], col_send.at[d], col_recv.at[me], place(d)
+        )
+
+    def round_own(part):
+        own_ref[part, :] = ctrl_ref[part, :].astype(jnp.bfloat16)
+
+    round_own(pl.ds(0, CHUNK))
     pl.semaphore_wait(barrier, devices - 1)
 
-    def request(dst, send, recv, other):
-        return pltpu.make_async_remote_copy(
-            src_ref=wanted_ref.at[0],
-            dst_ref=requested_ref.at[dst],
-            send_sem=want_send.at[send],
-            recv_sem=want_recv.at[recv],
-            device_id=place(other),
-            device_id_type=MESH,
-        )
-
     def ask(d, carry):
-        other = (me + d) % devices
-        request(me, other, me, other).start()
+        request(me, (me + d) % devices, me, (me + d) % devices).start()
         return carry
 
     lax.fori_loop(1, devices, ask, 0)
 
-    def swap(k):
-        part = pl.ds(cuts[k], cuts[k + 1] - cuts[k])
-        return pltpu.make_async_remote_copy(
-            src_ref=tile_ref.at[part],
-            dst_ref=swap_ref.at[part],
-            send_sem=swap_send.at[k],
-            recv_sem=swap_recv.at[k],
-            device_id=(partner, column),
-            device_id_type=MESH,
-        )
-
-    def forward(k):
-        part = pl.ds(cuts[k], cuts[k + 1] - cuts[k])
-        return pltpu.make_async_remote_copy(
-            src_ref=swap_ref.at[part],
-            dst_ref=far_ref.at[part],
-            send_sem=far_send.at[k],
-            recv_sem=far_recv.at[k],
-            device_id=(row + step, column),
-            device_id_type=MESH,
-        )
-
-    pieces = range(len(cuts) - 1)
-    for k in pieces:
-        swap(k).start()
-    requested_ref[me] = wanted_ref[0]
+    def send_own(k, carry):
+        round_own(chunk_of(k + 1))
+        swap(k, chunk_of(k)).start()
+        return carry
+
+    lax.fori_loop(0, full - 1, send_own, 0)
+    round_own(last)
+    swap(full - 1, chunk_of(full - 1)).start()
+    table_ref[me] = wanted_ref[0]
 
     @pl.when(jnp.logical_not(comes))
     def _():
         far_ref[...] = jnp.zeros_like(far_ref)
 
-    for k in pieces:
-        swap(k).wait_recv()
-
-        @pl.when(onward)
-        def _():
-            forward(k).start()
+    swap(full, last).start()
+
+    square = (GROUP, GROUP)
+    same = (iota(square, 0) >> log_lat) == (iota(square, 1) >> log_lat)
+    apart = (iota(square, 1) & (lat_rows - 1)) - (iota(square, 0) & (lat_rows - 1))
+
+    def lat_band(shift):
+        return halves(jnp.where(same, tap_value((apart + shift).astype(jnp.float32), LHALF), 0.0))
+
+    high, low = lat_band(0)
+    swap_high, swap_low = lat_band(lat_rows - 2 * lat_rows * odd)
+    far_high, far_low = lat_band(2 * lat_rows * odd - lat_rows)
+    for at, block in enumerate((high, high, low, swap_high, swap_low, far_high, far_low)):
+        band_ref[:, at * GROUP:(at + 1) * GROUP] = block
+    along = iota((lon_cols, lon_cols), 0) - iota((lon_cols, lon_cols), 1)
+    high, low = halves(tap_value(along.astype(jnp.float32), lon_half))
+    mid_ref[:, :lon_cols] = high
+    mid_ref[:, lon_cols:] = low
+    wide = (2 * lon_cols, 2 * lon_cols)
+    source, target = iota(wide, 0), iota(wide, 1)
+    within, which = source & (lon_half - 1), (source >> (log_lon - 1)) & 1
+    column_at = jnp.where(source < lon_cols, within - lon_half, within + lon_cols)
+    apart = column_at - (target & (lon_cols - 1))
+    value = jnp.where(which == (target >> log_lon), tap_value(apart.astype(jnp.float32), lon_half), 0.0)
+    high, low = halves(value)
+    edge_ref[0] = high
+    edge_ref[1] = low
+
+    def spread(c, carry):
+        std_row_ref[pl.ds(pl.multiple_of(c * lat_rows, lat_rows), lat_rows), :] = jnp.full(
+            (lat_rows, lon_cols), std_ref[0, c], jnp.float32
+        )
+        return carry
+
+    lax.fori_loop(0, width, spread, 0)
 
     def hear(d, carry):
         other = (me + d) % devices
@@ -161,40 +197,212 @@
         return carry
 
     lax.fori_loop(1, devices, hear, 0)
-    for k in pieces:
-        swap(k).wait_send()
-
-        @pl.when(comes)
-        def _():
-            forward(k).wait_recv()
+    listed = jnp.broadcast_to(table_ref[...].astype(jnp.float32), (devices, 8, table_ref.shape[2]))
+    wants = iota(listed.shape, 2) == iota(listed.shape, 1) + me * slots_each
+    cell = jnp.sum(jnp.where(wants, listed, 0.0), axis=2, keepdims=True).astype(jnp.int32)
+    cell = jnp.broadcast_to(cell, (devices, 8, lon_cols)).reshape(devices * 8, lon_cols)
+    row_ref[...] = cell >> log_lon
+    cell_ref[...] = jnp.where((cell & (lon_cols - 1)) == iota(cell.shape, 1), 1.0, 0.0).astype(jnp.bfloat16)
+
+    def lat_product(first, second):
+        def pair(ref):
+            return jnp.concatenate([ref[first, :], ref[second, :]], axis=1)
+
+        field = pair(ctrl_ref)
+        field_high, field_low = halves(field)
+        swapped, far = pair(swap_ref), pair(far_ref)
+        stacked = jnp.concatenate([field_high, field_low, field_high, swapped, swapped, far, far], axis=0)
+        return matmul(band_ref[...], stacked)
+
+    lane = iota((1, lon_cols), 1)
+
+    def pack(first, second, part):
+        right = jnp.where(lane < lon_half, pltpu.roll(first, lon_half, 1), second)
+        left = jnp.where(lane < lon_half, first, pltpu.roll(second, lon_half, 1))
+        to_right_ref[part, :] = right.astype(jnp.bfloat16)
+        to_left_ref[part, :] = left.astype(jnp.bfloat16)
+
+    def smooth_lat(k):
+        base = pl.multiple_of(k * CHUNK, CHUNK)
+        first, second = pl.ds(base, GROUP), pl.ds(base + GROUP, GROUP)
+        result = lat_product(first, second)
+        top, bottom = result[:, :lon_cols], result[:, lon_cols:]
+        g_ref[first, :] = top
+        g_ref[second, :] = bottom
+        pack(top, bottom, half_of(k))
+
+    def smooth_lat_last():
+        result = lat_product(pl.ds(rows - CHUNK, GROUP), pl.ds(rows - GROUP, GROUP))
+        kept = jnp.concatenate([result[:, :lon_cols], result[:, lon_cols:]], axis=0)[CHUNK - rest:]
+        g_ref[last, :] = kept
+        pack(kept[: rest // 2], kept[rest // 2:], last_half)
+
+    def smooth_lon(start, count, part):
+        half = count // 2
+        both = jnp.concatenate([from_left_ref[part, :], from_right_ref[part, :]], axis=1)
+        sides = matmul(both, edge_ref[0]) + matmul(both, edge_ref[1])
+        high, low = halves(g_ref[pl.ds(start, count), :])
+        own = matmul(high, mid_ref[...])
+        own = own[:, :lon_cols] + own[:, lon_cols:] + matmul(low, mid_ref[:, :lon_cols])
+        first, second = pl.ds(start, half), pl.ds(start + half, half)
+        inc_ref[first, :] = (own[:half] + sides[:, :lon_cols]) * std_row_ref[first, :]
+        inc_ref[second, :] = (own[half:] + sides[:, lon_cols:]) * std_row_ref[second, :]
+
+    def pick(start, count, group):
+        values = inc_ref[pl.ds(start, count), :].astype(jnp.bfloat16)
+        found = across(cell_ref[...], values)
+        mine = (iota(row_ref.shape, 1) & (lat_rows - 1)) == row_ref[...]
+        parts = []
+        for at in range(0, count, lon_cols):
+            piece = found[:, at:at + lon_cols]
+            parts.append(jnp.where(mine[:, : piece.shape[1]], piece, 0.0).astype(jnp.bfloat16))
+        masked = jnp.concatenate(parts, axis=1)
+        gather = (iota((count, lon_cols), 0) >> log_lat) == iota((count, lon_cols), 1)
+        result = matmul(masked, jnp.where(gather, 1.0, 0.0).astype(jnp.bfloat16))
+        result = result.reshape(devices, 8, lon_cols)[:, :slots_each, :]
+        pick_ref[:, :, pl.ds(pl.multiple_of(group * lon_cols, lon_cols), lon_cols)] = result.astype(jnp.bfloat16)
+
+    def send_back(group):
+        def give(d, carry):
+            back((me + d) % devices, group).start()
+            return carry
+
+        lax.fori_loop(1, devices, give, 0)
+
+    def stage(k, carry):
+        def arrive(k, part):
+            swap(k, part).wait_recv()
+
+            @pl.when(onward)
+            def _():
+                forward(k, part).start()
+
+        def await_far(k, part):
+            @pl.when(comes)
+            def _():
+                forward(k, part).wait_recv()
+
+        @pl.when(k < full)
+        def _():
+            arrive(k, chunk_of(k))
+
+        @pl.when(k == full)
+        def _():
+            arrive(full, last)
+
+        @pl.when(jnp.logical_and(k >= 1, k <= full))
+        def _():
+            await_far(k - 1, chunk_of(k - 1))
+            smooth_lat(k - 1)
+
+        @pl.when(k == full + 1)
+        def _():
+            await_far(full, last)
+            smooth_lat_last()
+
+        @pl.when(jnp.logical_and(k >= 2, k <= full + 1))
+        def _():
+            to_right(k - 2, half_of(k - 2)).wait_recv()
+            to_left(k - 2, half_of(k - 2)).wait_recv()
+            smooth_lon(pl.multiple_of((k - 2) * CHUNK, CHUNK), CHUNK, half_of(k - 2))
+
+        @pl.when(jnp.logical_and(k >= 1, k <= full))
+        def _():
+            to_right(k - 1, half_of(k - 1)).start()
+            to_left(k - 1, half_of(k - 1)).start()
+
+        @pl.when(k == full + 1)
+        def _():
+            to_right(full, last_half).start()
+            to_left(full, last_half).start()
+
+        @pl.when(jnp.logical_and(jnp.logical_and(k >= 3, k <= full + 1), k % 2 == 1))
+        def _():
+            group = k // 2 - 1
+            pick(pl.multiple_of(group * 2 * CHUNK, 2 * CHUNK), 2 * CHUNK, group)
+            send_back(group)
+
+        @pl.when(k == full + 2)
+        def _():
+            to_right(full, last_half).wait_recv()
+            to_left(full, last_half).wait_recv()
+            smooth_lon(full * CHUNK, rest, last_half)
+            pick(full * CHUNK, rest, full // 2)
+            send_back(full // 2)
+
+        return carry
+
+    lax.fori_loop(0, full + 3, stage, 0)
+    got_ref[me] = pick_ref[me]
+
+    def finish(k, part, half):
+        swap(k, part).wait_send()
 
         @pl.when(onward)
         def _():
-            forward(k).wait_send()
-
-
-def exchange(tile, wanted):
+            forward(k, part).wait_send()
+
+        to_right(k, half).wait_send()
+        to_left(k, half).wait_send()
+
+    def finish_full(k, carry):
+        finish(k, chunk_of(k), half_of(k))
+        return carry
+
+    lax.fori_loop(0, full, finish_full, 0)
+    finish(full, last, last_half)
+
+    def collect(d, carry):
+        other = (me + d) % devices
+        whole = remote(
+            pick_ref.at[other], got_ref.at[other], col_send.at[other], col_recv.at[other], place(other)
+        )
+        whole.wait_send()
+        whole.wait_recv()
+        return carry
+
+    lax.fori_loop(1, devices, collect, 0)
+
+
+def dense_step(control, wanted, std_dev, slots_each):
     lat, lon = lax.axis_size("lat"), lax.axis_size("lon")
-    devices, slots = lat * lon, wanted.shape[0]
-    width, pieces = tile.shape[0], 6
-    cuts = [width * k // pieces for k in range(pieces + 1)]
-    wanted = jnp.pad(wanted, (0, -slots % 128))[None, None, :]
+    width, lat_rows, lon_cols = control.shape
+    devices, rows = lat * lon, width * lat_rows
+    pieces = rows // CHUNK + 1
+    lanes = lane_tiles(width) * lon_cols
+    wanted = jnp.pad(wanted, (0, -wanted.shape[0] % 128))[None, None, :]
     vmem = pl.BlockSpec(memory_space=pltpu.VMEM)
     dma = pltpu.SemaphoreType.DMA
-    swapped, far, requested = pl.pallas_call(
-        functools.partial(exchange_kernel, lat, lon, cuts),
-        in_specs=[vmem, vmem],
+    bf16, f32 = jnp.bfloat16, jnp.float32
+    return pl.pallas_call(
+        functools.partial(dense_kernel, lat, lon, lat_rows, slots_each),
+        in_specs=[vmem, vmem, pl.BlockSpec(memory_space=pltpu.SMEM)],
         out_specs=[vmem, vmem, vmem],
         out_shape=[
-            jax.ShapeDtypeStruct(tile.shape, tile.dtype),
-            jax.ShapeDtypeStruct(tile.shape, tile.dtype),
+            jax.ShapeDtypeStruct((rows, lon_cols), f32),
             jax.ShapeDtypeStruct((devices, *wanted.shape[1:]), wanted.dtype),
+            jax.ShapeDtypeStruct((devices, slots_each, lanes), bf16),
         ],
-        scratch_shapes=[dma((pieces,))] * 4 + [dma((devices,))] * 2,
+        scratch_shapes=[
+            pltpu.VMEM((rows, lon_cols), bf16),
+            pltpu.VMEM((rows, lon_cols), bf16),
+            pltpu.VMEM((rows, lon_cols), bf16),
+            pltpu.VMEM((rows, lon_cols), f32),
+            *[pltpu.VMEM((rows // 2, lon_cols), bf16)] * 4,
+            pltpu.VMEM((GROUP, 7 * GROUP), bf16),
+            pltpu.VMEM((lon_cols, 2 * lon_cols), bf16),
+            pltpu.VMEM((2, 2 * lon_cols, 2 * lon_cols), bf16),
+            pltpu.VMEM((rows, lon_cols), f32),
+            pltpu.VMEM((devices * 8, lon_cols), bf16),
+            pltpu.VMEM((devices * 8, lon_cols), jnp.int32),
+            pltpu.VMEM((devices, slots_each, lanes), bf16),
+            *[dma((pieces,))] * 4,
+            *[dma((2, pieces))] * 2,
+            *[dma((devices,))] * 4,
+        ],
         compiler_params=pltpu.CompilerParams(collective_id=0, has_side_effects=True),
-        name="exchange",
-    )(tile, wanted)
-    return swapped, far, requested[:, 0, :slots]
+        name="dense",
+    )(control.reshape(rows, lon_cols), wanted, std_dev[None, :])
 
 
 def lane_tiles(count):
@@ -315,7 +523,8 @@
     order_in = jnp.sum(earlier * onehot, axis=1)
     slot = target * slots_each + order_in
     wanted = jnp.zeros((slots,), jnp.int32).at[slot].set(col_cell)
-    swapped, far, table = exchange(control.astype(jnp.bfloat16), wanted)
+    increment, table, got = dense_step(control, wanted, std_dev, slots_each)
+    increment, table = increment.reshape(control.shape), table[:, 0, :slots]
     lat_at, lon_at = lax.axis_index("lat"), lax.axis_index("lon")
     lat_devices, lon_devices = lax.axis_size("lat"), lax.axis_size("lon")
 
@@ -324,15 +533,7 @@
         owner = row * lon_devices + (lon_at + lon_shift) % lon_devices
         return lax.dynamic_slice(table, (0, owner * slots_each), (devices, slots_each))
 
-    requested = asked_of(0, 0).reshape(-1)
-
-    increment = smooth(control, swapped, far) * std_dev[:, None, None]
-    flat_field = increment.reshape(width, lat_rows * lon_cols)
-    picked = jnp.take(flat_field, requested, axis=1).T.astype(jnp.bfloat16)
-    returned = lax.all_to_all(
-        picked.reshape(devices, slots_each, width), ("lat", "lon"), split_axis=0, concat_axis=0, tiled=True
-    )
-    columns = returned.reshape(slots, width)[slot]
+    columns = got[:, :, :width].reshape(slots, width)[slot]
     departures, column_grad = sounding_step(jacobian, columns, innovation, inv_error)
     wide = column_grad.shape[1]
     outgoing = jnp.zeros((slots, wide), jnp.bfloat16).at[slot].set(column_grad)

time: 188 us -> 161 us (0.86)
  Pallas kernels: 68.1 us -> 91.2 us
  waiting for transfers between devices: 49.4 us -> 29.9 us
  matrix products: 12.5 us -> 0.89 us
  starting transfers between devices: 18.3 us -> 9.86 us
  local copies, waits for them, and re-layouts: 25.8 us -> 19.6 us
  other arithmetic: 8.94 us -> 4.13 us
    pallas_call x1, Pallas kernels: 40.1 us -> 63.4 us  [dense_step(): pl.pallas_call(functools.partial(dense_kernel, lat, lon, lat_rows, slots_...]
    dot_general x4 -> x0, matrix products: 12.4 us -> none  [the longest x1 5.49 us: smooth(): jnp.dot(field.reshape(width * lat_rows, lon_cols), lon_band[lon_half:-lon...]
    all_to_all x1 -> x0, waiting for transfers between devices: 9.28 us -> none  [local(): lax.all_to_all(picked.reshape(devices, slots_each, width), ('lat', 'lon')...]
    ppermute x2 -> x0, waiting for transfers between devices: 8.38 us -> none  [the longest x1 6.46 us: smooth(): right = lax.ppermute(paired(rounded[:, :, :lon_half]), 'lon', down)]
    convert_element_type x4 -> x0, other arithmetic: 4.49 us -> none  [the longest x1 2.74 us: local(): swapped, far, table = exchange(control.astype(jnp.bfloat16), wanted)]
    all_to_all x1 -> x0, starting transfers between devices: 3.48 us -> none  [local(): lax.all_to_all(picked.reshape(devices, slots_each, width), ('lat', 'lon')...]
    reshape x5 -> x1, local copies, waits for them, and re-layouts: 4.28 us -> 1.12 us  [local(): columns = got[:, :, :width].reshape(slots, width)[slot]]
    ppermute x4, starting transfers between devices: 9.63 us -> 6.59 us  [around(): return (lax.ppermute(array, axis, up), lax.ppermute(array, axis, down))]
  transfers between devices with their start and end apart: 8 -> 5, of which waited for: 7 -> 5; matrix products, arithmetic and copies ran while one was open for 6% -> 4% of each run, Pallas kernels for 0% -> 0%
where the time goes in v1:
time: 161 us; the launch traced here: 158 us
  Pallas kernels  91.2 us (57%)
  waiting for transfers between devices  29.9 us (19%)
  local copies, waits for them, and re-layouts  19.6 us (12%)
  starting transfers between devices  9.86 us (6%)
  other arithmetic  4.13 us (3%)
  between operations  2.33 us (1%)
    pallas_call x1, Pallas kernels, dense_step(): pl.pallas_call(functools.partial(dense_kernel, lat, lon, lat_rows, slots_...  63.4 us
    ppermute x4, waiting for transfers between devices, around(): return (lax.ppermute(array, axis, up), lax.ppermute(array, axis, down))  20.6 us
    pallas_call x1, Pallas kernels, sounding_step(): pl.pallas_call(functools.partial(sounding_kernel, channels, step), grid=(...  16.6 us
    pallas_call x1, Pallas kernels, adjoint_step(): pl.pallas_call(adjoint_kernel, grid=(lat_rows,), in_specs=[whole, whole,...  11.2 us
    all_to_all x1, waiting for transfers between devices, local(): lax.all_to_all(outgoing.reshape(devices, slots_each, wide), ('lat', 'lon'...  9.28 us
    unnamed x24, local copies, waits for them, and re-layouts  7.1 us
    ppermute x4, starting transfers between devices, around(): return (lax.ppermute(array, axis, up), lax.ppermute(array, axis, down))  6.59 us
    all_to_all x1, starting transfers between devices, local(): lax.all_to_all(outgoing.reshape(devices, slots_each, wide), ('lat', 'lon'...  3.27 us
  transfers between devices with their start and end apart: 5, of which 5 were waited for; matrix products, arithmetic and copies ran while one was open for 4% of the time, Pallas kernels for 0%

profile of v1, /device:TPU:2, one launch (start us, length us, event | category | flops | bytes accessed | tf_op | source)
XLA Modules:
  0.0 157.9 jit_solution(1266705061123415559)
XLA Ops:
  0.6 0.9 fusion.1
  1.5 0.7 fusion.20
  2.2 1.0 scatter_custom_fusion
  3.2 0.6 pad.12
  3.8 1.3 broadcast_in_dim.36.std_ref
  5.0 1.0 copy.43
  6.0 63.4 %dense.1 = (f32[4384,128]{1,0:T(8,128)}, s32[32,1,256]{2,1,0:T(1,128)}, bf16[32,6,640]{2,1,0:T(8,128)(2,1)}) custom-call(f32[4384,128]{1,0:T(8,128)} %bitcast.32, s32[1,1,256]{2,1,0:T(1,128)} %bitcast.46, f32[1,548]{1,0:T(1,128)} %broadcast_in_dim.36.std_ref), custom_call_target="tpu_custom_call" | custom-call | tf_op jit(solution)/shard_map/dense/pallas_call | solution.py:377
  69.4 1.1 reshape.281
  70.5 0.6 pad.13.innov_ref
  71.2 1.4 gather_fusion
  72.6 16.6 %soundings.1 = (f32[96,256]{1,0:T(8,128)}, bf16[96,640]{1,0:T(8,128)(2,1)}) custom-call(bf16[150,96,548]{2,1,0:T(8,128)(2,1)} %bitcast.29, bf16[96,548]{1,0:T(8,128)(2,1)} %gather_fusion, f32[96,256]{1,0:T(8,128)} %pad.13.innov_ref, f32[1,150]{1,0:T(1,128)} %bitcast.47), custom_call_target="tpu_custom_call" | custom-call | tf_op jit(solution)/shard_map/soundings/pallas_call | solution.py:450
  89.2 0.0 copy-start.5
  89.2 1.4 scatter_custom_fusion.1
  90.7 0.0 copy-start.7
  90.7 0.8 reshape.283
  91.5 3.3 %all-to-all-start = ((bf16[32,6,640]{2,1,0:T(8,128)(2,1)}), bf16[32,6,640]{2,1,0:T(8,128)(2,1)S(1)}, u32[]{:S(2)}, u32[]{:S(2)}) async-start(bf16[32,6,640]{2,1,0:T(8,128)(2,1)} %reshape.283), calls=%async_computation | async-start | bytes 655360 | tf_op jit(solution)/shard_map/all_to_all | solution.py:540
  94.9 0.0 copy-done.4
  94.9 0.4 constant_dynamic-slice_fusion.8
  95.3 0.1 copy.54
  95.4 0.1 copy.53
  95.5 0.1 copy.52
  95.5 9.3 %all-to-all-done = bf16[32,6,640]{2,1,0:T(8,128)(2,1)S(1)} async-done(((bf16[32,6,640]{2,1,0:T(8,128)(2,1)}), bf16[32,6,640]{2,1,0:T(8,128)(2,1)S(1)}, u32[]{:S(2)}, u32[]{:S(2)}) %all-to-all-start) | async-done | bytes 245792 | tf_op jit(solution)/shard_map/all_to_all | solution.py:540
  104.8 0.1 reshape.284
  104.9 4.1 %collective-permute-start = (bf16[192,640]{1,0:T(8,128)(2,1)S(1)}, bf16[192,640]{1,0:T(8,128)(2,1)S(1)}, u32[]{:S(2)}, u32[]{:S(2)}) collective-permute-start(bf16[192,640]{1,0:T(8,128)(2,1)S(1)} %reshape.284), channel_id=1, source_target_pairs={{0,8},{8,16},{16,24},{1,9},{9,17},{17,25},{2,10},{10,18},{18,26},{... | collective-permute-start | bytes 737288 | tf_op jit(solution)/shard_map/ppermute | solution.py:32
  109.1 0.1 copy.50
  109.1 0.1 copy.49
  109.2 0.1 copy.48
  109.3 1.9 %collective-permute-start.1 = (bf16[192,640]{1,0:T(8,128)(2,1)S(1)}, bf16[192,640]{1,0:T(8,128)(2,1)S(1)}, u32[]{:S(2)}, u32[]{:S(2)}) collective-permute-start(bf16[192,640]{1,0:T(8,128)(2,1)S(1)} %reshape.284), channel_id=1, source_target_pairs={{8,0},{16,8},{24,16},{9,1},{17,9},{25,17},{10,2},{18,10},{26,18},{... | collective-permute-start | bytes 737288 | tf_op jit(solution)/shard_map/ppermute | solution.py:32
  111.2 0.1 copy.44
  111.3 0.1 copy.46
  111.4 0.1 copy.45
  111.5 3.9 %collective-permute-done = bf16[192,640]{1,0:T(8,128)(2,1)S(1)} collective-permute-done((bf16[192,640]{1,0:T(8,128)(2,1)S(1)}, bf16[192,640]{1,0:T(8,128)(2,1)S(1)}, u32[]{:S(2)}, u32[]{:S(2)}) %collective-permute-start) | collective-permute-done | bytes 245792 | tf_op jit(solution)/shard_map/ppermute | solution.py:32
  115.5 5.6 %collective-permute-done.1 = bf16[192,640]{1,0:T(8,128)(2,1)S(1)} collective-permute-done((bf16[192,640]{1,0:T(8,128)(2,1)S(1)}, bf16[192,640]{1,0:T(8,128)(2,1)S(1)}, u32[]{:S(2)}, u32[]{:S(2)}) %collective-permute-start.1) | collective-permute-done | bytes 245792 | tf_op jit(solution)/shard_map/ppermute | solution.py:32
  121.1 0.0 copy-start.1
  121.1 0.1 collective-permute-start.3
  121.2 0.5 collective-permute-start.2
  121.7 0.0 copy-done.6
  121.7 0.6 fusion.19
  123.0 0.6 fusion.16
  124.3 0.0 copy-done.8
  124.3 0.1 add.190
  124.4 0.1 add.191
  124.5 0.6 broadcast_in_dim.41.std_ref
  125.1 0.0 copy-done.5
  125.1 0.7 copy.56
  125.8 0.1 copy.47
  125.9 0.1 stack.52
  126.1 0.1 copy.51
  126.2 0.1 stack.57
  126.3 0.1 copy.55
  126.4 0.1 stack.62
  126.6 0.0 copy-done.7
  126.6 0.1 fusion.11
  126.7 0.8 compare_select_fusion.row_ref
  127.5 1.3 fusion.5.col_ref
  128.8 8.8 %collective-permute-done.3.after_ref = bf16[576,640]{1,0:T(8,128)(2,1)S(1)} collective-permute-done((bf16[576,640]{1,0:T(8,128)(2,1)S(1)}, bf16[576,640]{1,0:T(8,128)(2,1)S(1)}, u32[]{:S(2)}, u32[]{:S(2)}) %collective-permute-start.3) | collective-permute-done | bytes 737312 | tf_op jit(solution)/shard_map/ppermute | solution.py:32
  137.5 2.3 %collective-permute-done.2.before_ref = bf16[576,640]{1,0:T(8,128)(2,1)S(1)} collective-permute-done((bf16[576,640]{1,0:T(8,128)(2,1)S(1)}, bf16[576,640]{1,0:T(8,128)(2,1)S(1)}, u32[]{:S(2)}, u32[]{:S(2)}) %collective-permute-start.2) | collective-permute-done | bytes 737312 | tf_op jit(solution)/shard_map/ppermute | solution.py:32
  139.8 0.0 copy-done.1
  139.9 0.9 copy-done.3
  140.7 11.2 %adjoint.1 = f32[548,1024]{1,0:T(8,128)} custom-call(bf16[576,640]{1,0:T(8,128)(2,1)} %copy-done.1, bf16[576,640]{1,0:T(8,128)(2,1)} %copy-done.3, bf16[576,640]{1,0:T(8,128)(2,1)} %copy-done.2, f32[3,128,576]{2,1,0:T(8,128)} %fusion.5.col_ref, f32[8,3,1,576]{3,2,1,0:T(1,128)} %compare_select_fusion.row_ref, f32[1,640]{1,0:T(1,128)} %broadcast_in_dim.41.std_ref), custom_call_target="tpu_custom_call" | custom-call | tf_op jit(solution)/shard_map/adjoint/pallas_call | solution.py:493
  152.0 2.1 %copy.57 = f32[69,8,8,128]{3,2,1,0:T(8,128)S(1)} copy(f32[69,8,8,128]{3,1,2,0:T(8,128)} %bitcast.30) | data formatting | bytes 4521984
  154.1 1.5 slice.14
  155.6 0.9 copy-done
  156.6 1.4 copy.61
  (15 shorter events, 0.2 us)
Async XLA Ops:
  72.6 22.3 %copy-start.4 = (s32[32,1,256]{2,1,0:T(1,128)S(1)}, s32[32,1,256]{2,1,0:T(1,128)}, u32[]{:S(2)}) copy-start(s32[32,1,256]{2,1,0:T(1,128)} %get-tuple-element.12) | copy-start | bytes 98308
  89.2 32.5 %copy-start.6 = (f32[548]{0:T(1024)S(1)}, f32[548]{0:T(1024)}, u32[]{:S(2)}) copy-start(f32[548]{0:T(1024)} %param.9) | copy-start | bytes 6580
  89.2 35.1 %copy-start.8 = (s32[3]{0:T(128)S(1)}, s32[3]{0:T(128)}, u32[]{:S(2)}) copy-start(s32[3]{0:T(128)} %constant.129) | copy-start | bytes 40
  89.2 35.9 %copy-start.5 = (f32[96,256]{1,0:T(8,128)S(1)}, f32[96,256]{1,0:T(8,128)}, u32[]{:S(2)}) copy-start(f32[96,256]{1,0:T(8,128)} %get-tuple-element.9) | copy-start | bytes 294916
  90.7 35.9 %copy-start.7 = (s32[3]{0:T(128)S(1)}, s32[3]{0:T(128)}, u32[]{:S(2)}) copy-start(s32[3]{0:T(128)} %constant.128) | copy-start | bytes 40
  91.5 13.3 %all-to-all-start = ((bf16[32,6,640]{2,1,0:T(8,128)(2,1)}), bf16[32,6,640]{2,1,0:T(8,128)(2,1)S(1)}, u32[]{:S(2)}, u32[]{:S(2)}) async-start(bf16[32,6,640]{2,1,0:T(8,128)(2,1)} %reshape.283), calls=%async_computation | async-start | bytes 655360 | tf_op jit(solution)/shard_map/all_to_all | solution.py:540
  104.9 10.5 %collective-permute-start = (bf16[192,640]{1,0:T(8,128)(2,1)S(1)}, bf16[192,640]{1,0:T(8,128)(2,1)S(1)}, u32[]{:S(2)}, u32[]{:S(2)}) collective-permute-start(bf16[192,640]{1,0:T(8,128)(2,1)S(1)} %reshape.284), channel_id=1, source_target_pairs={{0,8},{8,16},{16,24},{1,9},{9,17},{17,25},{2,10},{10,18},{18,26},{... | collective-permute-start | bytes 737288 | tf_op jit(solution)/shard_map/ppermute | solution.py:32
  109.3 11.8 %collective-permute-start.1 = (bf16[192,640]{1,0:T(8,128)(2,1)S(1)}, bf16[192,640]{1,0:T(8,128)(2,1)S(1)}, u32[]{:S(2)}, u32[]{:S(2)}) collective-permute-start(bf16[192,640]{1,0:T(8,128)(2,1)S(1)} %reshape.284), channel_id=1, source_target_pairs={{8,0},{16,8},{24,16},{9,1},{17,9},{25,17},{10,2},{18,10},{26,18},{... | collective-permute-start | bytes 737288 | tf_op jit(solution)/shard_map/ppermute | solution.py:32
  121.1 18.7 %copy-start.1 = (bf16[576,640]{1,0:T(8,128)(2,1)}, bf16[576,640]{1,0:T(8,128)(2,1)S(1)}, u32[]{:S(2)}) copy-start(bf16[576,640]{1,0:T(8,128)(2,1)S(1)} %constant_dynamic-update-slice_fusion.near_ref) | copy-start | bytes 2211844
  121.1 16.4 %collective-permute-start.3 = (bf16[576,640]{1,0:T(8,128)(2,1)S(1)}, bf16[576,640]{1,0:T(8,128)(2,1)S(1)}, u32[]{:S(2)}, u32[]{:S(2)}) collective-permute-start(bf16[576,640]{1,0:T(8,128)(2,1)S(1)} %constant_dynamic-update-slice_fusion.near_ref), channel_id=1, source_target_pairs={{1,0},{2,1},{3,2},{4,3},{5,4},{6,5},{7,6},{0,7},{9,8},{10,9},{11,1... | collective-permute-start | bytes 2211848 | tf_op jit(solution)/shard_map/ppermute | solution.py:32
  121.2 18.7 %collective-permute-start.2 = (bf16[576,640]{1,0:T(8,128)(2,1)S(1)}, bf16[576,640]{1,0:T(8,128)(2,1)S(1)}, u32[]{:S(2)}, u32[]{:S(2)}) collective-permute-start(bf16[576,640]{1,0:T(8,128)(2,1)S(1)} %constant_dynamic-update-slice_fusion.near_ref), channel_id=1, source_target_pairs={{0,1},{1,2},{2,3},{3,4},{4,5},{5,6},{6,7},{7,0},{8,9},{9,10},{10,1... | collective-permute-start | bytes 2211848 | tf_op jit(solution)/shard_map/ppermute | solution.py:32
  137.5 2.3 %copy-start.2 = (bf16[576,640]{1,0:T(8,128)(2,1)}, bf16[576,640]{1,0:T(8,128)(2,1)S(1)}, u32[]{:S(2)}) copy-start(bf16[576,640]{1,0:T(8,128)(2,1)S(1)} %collective-permute-done.3.after_ref) | copy-start | bytes 2211844
  139.9 0.9 copy-start.3
  154.1 2.4 %copy-start = (f32[4384,128]{1,0:T(8,128)S(1)}, f32[4384,128]{1,0:T(8,128)}, u32[]{:S(2)}) copy-start(f32[4384,128]{1,0:T(8,128)} %get-tuple-element.10) | copy-start | bytes 6733828

commit v2 on v1

v2 whole, which is shorter than its diff:
```python
import functools
import math

import jax
import jax.numpy as jnp
from jax import lax
from jax.experimental import pallas as pl
from jax.experimental.pallas import tpu as pltpu
from jax.sharding import PartitionSpec as P

LHALF = 8
MESH = pl.DeviceIdType.MESH


def tap_weights(offset, half_width):
    spread = 2.0 * half_width / 3.0
    taps = jnp.arange(-half_width, half_width + 1, dtype=jnp.int32).astype(jnp.float32)
    norm_total = jnp.sqrt(jnp.sum(jnp.exp(-taps * taps / (spread * spread))))
    weights = jnp.exp(-offset * offset / (2.0 * spread * spread)) / norm_total
    return jnp.where(jnp.abs(offset) <= half_width, weights, jnp.zeros_like(weights))


def halves(weights):
    high = weights.astype(jnp.bfloat16)
    return high, (weights - high.astype(jnp.float32)).astype(jnp.bfloat16)


def tap_value(offset, half_width):
    spread = 2.0 * half_width / 3.0
    norm_total = math.sqrt(sum(math.exp(-e * e / (spread * spread)) for e in range(-half_width, half_width + 1)))
    weights = jnp.exp(-offset * offset / (2.0 * spread * spread)) / norm_total
    return jnp.where(jnp.abs(offset) <= half_width, weights, 0.0)


GROUP = 256
CHUNK = 2 * GROUP


def matmul(left, right):
    return jnp.dot(left, right, preferred_element_type=jnp.float32)


def across(left, right):
    return lax.dot_general(left, right, (((1,), (1,)), ((), ())), preferred_element_type=jnp.float32)


def slots_of(dev_ref, cell_ref, slots_each, count):
    sound_count = dev_ref.shape[1]
    square = (sound_count, sound_count)
    iota = lambda shape, axis: lax.broadcasted_iota(jnp.int32, shape, axis)
    before = iota(square, 0) - iota(square, 1)
    across_lanes = jnp.broadcast_to(dev_ref[...].astype(jnp.float32), square)
    upright = lambda spread: jnp.sum(jnp.where(before == 0, spread, 0.0), axis=1, keepdims=True)
    down = upright(across_lanes)
    alike = across_lanes == down
    order = jnp.sum(jnp.where(jnp.logical_and(alike, before > 0), 1.0, 0.0), axis=1, keepdims=True)
    slot = down * slots_each + order
    onehot = slot.astype(jnp.int32) == iota((sound_count, count), 1)
    cell = upright(jnp.broadcast_to(cell_ref[...].astype(jnp.float32), square))
    order = jnp.sum(jnp.where(jnp.logical_and(alike, before < 0), 1.0, 0.0), axis=0, keepdims=True)
    return onehot, cell, (dev_ref[...].astype(jnp.float32) * slots_each + order).astype(jnp.int32)


def dense_kernel(
    lat, lon, lat_rows, slots_each,
    ctrl_hbm, dev_ref, ask_ref, std_ref,
    inc_hbm, table_ref, got_ref,
    ctrl_ref, inc_ref, wanted_ref, own_ref, swap_ref, far_ref, g_ref, to_right_ref, to_left_ref, from_left_ref, from_right_ref,
    band_ref, mid_ref, edge_ref, std_row_ref, cell_ref, row_ref, pick_ref,
    swap_send, swap_recv, far_send, far_recv, lon_send, lon_recv,
    want_send, want_recv, col_send, col_recv, load_sem, store_sem,
):
    rows, lon_cols = ctrl_ref.shape
    width = rows // lat_rows
    full, rest = rows // CHUNK, rows % CHUNK
    early = full // 4 * 2
    log_lat, log_lon = lat_rows.bit_length() - 1, lon_cols.bit_length() - 1
    lon_half = lon_cols // 2
    row, column = lax.axis_index("lat"), lax.axis_index("lon")
    devices, me = lat * lon, row * lon + column
    odd = row % 2
    partner, step = row + 1 - 2 * odd, 2 - 4 * odd
    onward = jnp.logical_and(row + step >= 0, row + step < lat)
    comes = jnp.logical_and(row - step >= 0, row - step < lat)
    place = lambda other: (other // lon, other % lon)
    iota = lambda shape, axis: lax.broadcasted_iota(jnp.int32, shape, axis)

    barrier = pltpu.get_barrier_semaphore()

    def greet(d, carry):
        pl.semaphore_signal(barrier, inc=1, device_id=place((me + d) % devices), device_id_type=MESH)
        return carry

    lax.fori_loop(1, devices, greet, 0)

    def chunk_of(k):
        return pl.ds(pl.multiple_of(k * CHUNK, CHUNK), CHUNK)

    def half_of(k):
        return pl.ds(pl.multiple_of(k * GROUP, GROUP), GROUP)

    last, last_half = pl.ds(full * CHUNK, rest), pl.ds(full * GROUP, rest // 2)

    def remote(source, target, send, recv, device):
        return pltpu.make_async_remote_copy(
            src_ref=source, dst_ref=target, send_sem=send, recv_sem=recv, device_id=device, device_id_type=MESH
        )

    def request(dst, send, recv, other):
        return remote(wanted_ref.at[0], table_ref.at[dst], want_send.at[send], want_recv.at[recv], place(other))

    def swap(k, part):
        return remote(own_ref.at[part], swap_ref.at[part], swap_send.at[k], swap_recv.at[k], (partner, column))

    def forward(k, part):
        return remote(swap_ref.at[part], far_ref.at[part], far_send.at[k], far_recv.at[k], (row + step, column))

    def to_right(k, part):
        return remote(
            to_right_ref.at[part], from_left_ref.at[part], lon_send.at[0, k], lon_recv.at[0, k],
            (row, (column + 1) % lon),
        )

    def to_left(k, part):
        return remote(
            to_left_ref.at[part], from_right_ref.at[part], lon_send.at[1, k], lon_recv.at[1, k],
            (row, (column + lon - 1) % lon),
        )

    def back(d, group):
        part = pl.ds(pl.multiple_of(group * lon_cols, lon_cols), lon_cols)
        return remote(
            pick_ref.at[d, :, part], got_ref.at[me, :, part], col_send.at[d], col_recv.at[me], place(d)
        )

    def round_own(part):
        own_ref[part, :] = ctrl_ref[part, :].astype(jnp.bfloat16)

    def load(k, part):
        return pltpu.make_async_copy(ctrl_hbm.at[part], ctrl_ref.at[part], load_sem.at[k])

    def store(k, part):
        return pltpu.make_async_copy(inc_ref.at[part], inc_hbm.at[part], store_sem.at[k])

    def begin(k, carry):
        load(k, chunk_of(k)).start()
        return carry

    lax.fori_loop(0, full, begin, 0)
    load(full, last).start()
    onehot, cell_at, _ = slots_of(dev_ref, ask_ref, slots_each, wanted_ref.shape[2])
    wanted_ref[0] = jnp.sum(jnp.where(onehot, cell_at, 0.0), axis=0, keepdims=True).astype(jnp.int32)

    @pl.when(jnp.logical_not(comes))
    def _():
        far_ref[...] = jnp.zeros_like(far_ref)

    load(0, chunk_of(0)).wait()
    round_own(chunk_of(0))
    pl.semaphore_wait(barrier, devices - 1)

    def ask(d, carry):
        request(me, (me + d) % devices, me, (me + d) % devices).start()
        return carry

    lax.fori_loop(1, devices, ask, 0)

    def send_own(k, carry):
        load(k + 1, chunk_of(k + 1)).wait()

        @pl.when(k + 1 < early)
        def _():
            round_own(chunk_of(k + 1))

        swap(k, chunk_of(k)).start()
        return carry

    lax.fori_loop(0, early, send_own, 0)
    lane = iota((1, lon_cols), 1)

    def pack(first, second, part):
        right = jnp.where(lane < lon_half, pltpu.roll(first, lon_half, 1), second)
        left = jnp.where(lane < lon_half, first, pltpu.roll(second, lon_half, 1))
        to_right_ref[part, :] = right.astype(jnp.bfloat16)
        to_left_ref[part, :] = left.astype(jnp.bfloat16)

    def send_lon(k, part):
        to_right(k, part).start()
        to_left(k, part).start()

    def pack_own(k, carry):
        base = pl.multiple_of(k * CHUNK, CHUNK)
        pack(ctrl_ref[pl.ds(base, GROUP), :], ctrl_ref[pl.ds(base + GROUP, GROUP), :], half_of(k))

        @pl.when(k + 1 < full)
        def _():
            load(k + 1, chunk_of(k + 1)).wait()

        send_lon(k, half_of(k))
        return carry

    lax.fori_loop(early, full, pack_own, 0)
    load(full, last).wait()
    middle = full * CHUNK + rest // 2
    pack(ctrl_ref[full * CHUNK:middle, :], ctrl_ref[middle:, :], last_half)
    table_ref[me] = wanted_ref[0]
    send_lon(full, last_half)

    square = (GROUP, GROUP)
    same = (iota(square, 0) >> log_lat) == (iota(square, 1) >> log_lat)
    apart = (iota(square, 1) & (lat_rows - 1)) - (iota(square, 0) & (lat_rows - 1))

    def lat_band(shift):
        return halves(jnp.where(same, tap_value((apart + shift).astype(jnp.float32), LHALF), 0.0))

    high, low = lat_band(0)
    swap_high, swap_low = lat_band(lat_rows - 2 * lat_rows * odd)
    far_high, far_low = lat_band(2 * lat_rows * odd - lat_rows)
    for at, block in enumerate((high, high, low, swap_high, swap_low, far_high, far_low)):
        band_ref[:, at * GROUP:(at + 1) * GROUP] = block
    along = iota((lon_cols, lon_cols), 0) - iota((lon_cols, lon_cols), 1)
    high, low = halves(tap_value(along.astype(jnp.float32), lon_half))
    mid_ref[:, :lon_cols] = high
    mid_ref[:, lon_cols:] = low
    wide = (2 * lon_cols, 2 * lon_cols)
    source, target = iota(wide, 0), iota(wide, 1)
    within, which = source & (lon_half - 1), (source >> (log_lon - 1)) & 1
    column_at = jnp.where(source < lon_cols, within - lon_half, within + lon_cols)
    apart = column_at - (target & (lon_cols - 1))
    value = jnp.where(which == (target >> log_lon), tap_value(apart.astype(jnp.float32), lon_half), 0.0)
    high, low = halves(value)
    edge_ref[0] = high
    edge_ref[1] = low

    def spread(c, carry):
        std_row_ref[pl.ds(pl.multiple_of(c * lat_rows, lat_rows), lat_rows), :] = jnp.full(
            (lat_rows, lon_cols), std_ref[0, c], jnp.float32
        )
        return carry

    lax.fori_loop(0, width, spread, 0)

    def hear(d, carry):
        other = (me + d) % devices
        asked = request(other, other, other, other)
        asked.wait_send()
        asked.wait_recv()
        return carry

    lax.fori_loop(1, devices, hear, 0)
    listed = jnp.broadcast_to(table_ref[...].astype(jnp.float32), (devices, 8, table_ref.shape[2]))
    wants = iota(listed.shape, 2) == iota(listed.shape, 1) + me * slots_each
    cell = jnp.sum(jnp.where(wants, listed, 0.0), axis=2, keepdims=True).astype(jnp.int32)
    cell = jnp.broadcast_to(cell, (devices, 8, lon_cols)).reshape(devices * 8, lon_cols)
    row_ref[...] = cell >> log_lon
    cell_ref[...] = jnp.where((cell & (lon_cols - 1)) == iota(cell.shape, 1), 1.0, 0.0).astype(jnp.bfloat16)

    def lat_product(ref, first, second):
        def pair(ref):
            return jnp.concatenate([ref[first, :], ref[second, :]], axis=1)

        field = pair(ref)
        field_high, field_low = halves(field)
        swapped, far = pair(swap_ref), pair(far_ref)
        stacked = jnp.concatenate([field_high, field_low, field_high, swapped, swapped, far, far], axis=0)
        return matmul(band_ref[...], stacked)

    def lat_then_send(k):
        base = pl.multiple_of(k * CHUNK, CHUNK)
        first, second = pl.ds(base, GROUP), pl.ds(base + GROUP, GROUP)
        result = lat_product(ctrl_ref, first, second)
        top, bottom = result[:, :lon_cols], result[:, lon_cols:]
        g_ref[first, :] = top
        g_ref[second, :] = bottom
        pack(top, bottom, half_of(k))

    def lat_last(k):
        base = pl.multiple_of(k * CHUNK, CHUNK)
        first, second = pl.ds(base, GROUP), pl.ds(base + GROUP, GROUP)
        result = lat_product(g_ref, first, second)
        inc_ref[first, :] = result[:, :lon_cols] * std_row_ref[first, :]
        inc_ref[second, :] = result[:, lon_cols:] * std_row_ref[second, :]

    def lat_rest():
        result = lat_product(g_ref, pl.ds(rows - CHUNK, GROUP), pl.ds(rows - GROUP, GROUP))
        kept = jnp.concatenate([result[:, :lon_cols], result[:, lon_cols:]], axis=0)[CHUNK - rest:]
        inc_ref[last, :] = kept * std_row_ref[last, :]

    def lon_product(ref, start, count, part):
        half = count // 2
        both = jnp.concatenate([from_left_ref[part, :], from_right_ref[part, :]], axis=1)
        sides = matmul(both, edge_ref[0]) + matmul(both, edge_ref[1])
        high, low = halves(ref[pl.ds(start, count), :])
        own = matmul(high, mid_ref[...])
        own = own[:, :lon_cols] + own[:, lon_cols:] + matmul(low, mid_ref[:, :lon_cols])
        return own[:half] + sides[:, :lon_cols], own[half:] + sides[:, lon_cols:]

    def lon_last(k):
        base = pl.multiple_of(k * CHUNK, CHUNK)
        first, second = pl.ds(base, GROUP), pl.ds(base + GROUP, GROUP)
        top, bottom = lon_product(g_ref, base, CHUNK, half_of(k))
        inc_ref[first, :] = top * std_row_ref[first, :]
        inc_ref[second, :] = bottom * std_row_ref[second, :]

    def lon_first(start, count, part):
        first, second = pl.ds(start, count // 2), pl.ds(start + count // 2, count // 2)
        top, bottom = lon_product(ctrl_ref, start, count, part)
        g_ref[first, :] = top
        g_ref[second, :] = bottom
        own_ref[first, :] = top.astype(jnp.bfloat16)
        own_ref[second, :] = bottom.astype(jnp.bfloat16)

    def pick(start, count, group):
        values = inc_ref[pl.ds(start, count), :].astype(jnp.bfloat16)
        found = across(cell_ref[...], values)
        mine = (iota(row_ref.shape, 1) & (lat_rows - 1)) == row_ref[...]
        parts = []
        for at in range(0, count, lon_cols):
            piece = found[:, at:at + lon_cols]
            parts.append(jnp.where(mine[:, : piece.shape[1]], piece, 0.0).astype(jnp.bfloat16))
        masked = jnp.concatenate(parts, axis=1)
        gather = (iota((count, lon_cols), 0) >> log_lat) == iota((count, lon_cols), 1)
        result = matmul(masked, jnp.where(gather, 1.0, 0.0).astype(jnp.bfloat16))
        result = result.reshape(devices, 8, lon_cols)[:, :slots_each, :]
        pick_ref[:, :, pl.ds(pl.multiple_of(group * lon_cols, lon_cols), lon_cols)] = result.astype(jnp.bfloat16)

    def send_back(group):
        def give(d, carry):
            back((me + d) % devices, group).start()
            return carry

        lax.fori_loop(1, devices, give, 0)

    def stage(k, carry):
        def arrive(k, part):
            swap(k, part).wait_recv()

            @pl.when(onward)
            def _():
                forward(k, part).start()

        def await_far(k, part):
            @pl.when(comes)
            def _():
                forward(k, part).wait_recv()

        @pl.when(k < full)
        def _():
            arrive(k, chunk_of(k))

        @pl.when(k == full)
        def _():
            arrive(full, last)

        def await_lon(k, part):
            to_right(k, part).wait_recv()
            to_left(k, part).wait_recv()

        ahead, behind, done = k + early, k - 2, k - 4

        @pl.when(ahead < full)
        def _():
            await_lon(ahead, half_of(ahead))
            lon_first(pl.multiple_of(ahead * CHUNK, CHUNK), CHUNK, half_of(ahead))
            swap(ahead, chunk_of(ahead)).start()

        @pl.when(ahead == full)
        def _():
            await_lon(full, last_half)
            lon_first(full * CHUNK, rest, last_half)
            swap(full, last).start()

        @pl.when(jnp.logical_and(behind >= 0, behind < early))
        def _():
            await_far(behind, chunk_of(behind))
            lat_then_send(behind)

        @pl.when(jnp.logical_and(done >= 0, done < early))
        def _():
            await_lon(done, half_of(done))
            lon_last(done)
            store(done, chunk_of(done)).start()

        @pl.when(jnp.logical_and(behind >= 0, behind < early))
        def _():
            send_lon(behind, half_of(behind))

        @pl.when(jnp.logical_and(behind >= early, behind < full))
        def _():
            await_far(behind, chunk_of(behind))
            lat_last(behind)
            store(behind, chunk_of(behind)).start()

        def give(group):
            pick(pl.multiple_of(group * 2 * CHUNK, 2 * CHUNK), 2 * CHUNK, group)
            send_back(group)

        @pl.when(jnp.logical_and(jnp.logical_and(done >= 0, done < early), done % 2 == 1))
        def _():
            give(done // 2)

        @pl.when(jnp.logical_and(jnp.logical_and(behind >= early, behind < full), behind % 2 == 1))
        def _():
            give(behind // 2)

        @pl.when(behind == full)
        def _():
            await_far(full, last)
            lat_rest()
            store(full, last).start()
            pick(full * CHUNK, rest, full // 2)
            send_back(full // 2)

        return carry

    lax.fori_loop(0, full + 3, stage, 0)
    got_ref[me] = pick_ref[me]

    def finish(k, part, half):
        swap(k, part).wait_send()

        @pl.when(onward)
        def _():
            forward(k, part).wait_send()

        store(k, part).wait()
        to_right(k, half).wait_send()
        to_left(k, half).wait_send()

    def finish_full(k, carry):
        finish(k, chunk_of(k), half_of(k))
        return carry

    lax.fori_loop(0, full, finish_full, 0)
    finish(full, last, last_half)

    def collect(d, carry):
        other = (me + d) % devices
        whole = remote(
            pick_ref.at[other], got_ref.at[other], col_send.at[other], col_recv.at[other], place(other)
        )
        whole.wait_send()
        whole.wait_recv()
        return carry

    lax.fori_loop(1, devices, collect, 0)


def dense_step(control, col_dev, col_cell, std_dev, slots_each):
    lat, lon = lax.axis_size("lat"), lax.axis_size("lon")
    width, lat_rows, lon_cols = control.shape
    devices, rows = lat * lon, width * lat_rows
    pieces = rows // CHUNK + 1
    lanes = lane_tiles(width) * lon_cols
    listed = (1, lane_tiles(devices * slots_each) * 128)
    vmem, hbm = pl.BlockSpec(memory_space=pltpu.VMEM), pl.BlockSpec(memory_space=pl.ANY)
    dma = pltpu.SemaphoreType.DMA
    bf16, f32 = jnp.bfloat16, jnp.float32
    return pl.pallas_call(
        functools.partial(dense_kernel, lat, lon, lat_rows, slots_each),
        in_specs=[hbm, vmem, vmem, pl.BlockSpec(memory_space=pltpu.SMEM)],
        out_specs=[hbm, vmem, vmem],
        out_shape=[
            jax.ShapeDtypeStruct((rows, lon_cols), f32),
            jax.ShapeDtypeStruct((devices, *listed), jnp.int32),
            jax.ShapeDtypeStruct((devices, slots_each, lanes), bf16),
        ],
        scratch_shapes=[
            pltpu.VMEM((rows, lon_cols), f32),
            pltpu.VMEM((rows, lon_cols), f32),
            pltpu.VMEM((1, *listed), jnp.int32),
            pltpu.VMEM((rows, lon_cols), bf16),
            pltpu.VMEM((rows, lon_cols), bf16),
            pltpu.VMEM((rows, lon_cols), bf16),
            pltpu.VMEM((rows, lon_cols), f32),
            *[pltpu.VMEM((rows // 2, lon_cols), bf16)] * 4,
            pltpu.VMEM((GROUP, 7 * GROUP), bf16),
            pltpu.VMEM((lon_cols, 2 * lon_cols), bf16),
            pltpu.VMEM((2, 2 * lon_cols, 2 * lon_cols), bf16),
            pltpu.VMEM((rows, lon_cols), f32),
            pltpu.VMEM((devices * 8, lon_cols), bf16),
            pltpu.VMEM((devices * 8, lon_cols), jnp.int32),
            pltpu.VMEM((devices, slots_each, lanes), bf16),
            *[dma((pieces,))] * 4,
            *[dma((2, pieces))] * 2,
            *[dma((devices,))] * 4,
            *[dma((pieces,))] * 2,
        ],
        compiler_params=pltpu.CompilerParams(collective_id=0, has_side_effects=True),
        name="dense",
    )(control.reshape(rows, lon_cols), col_dev.reshape(1, -1), col_cell[None, :], std_dev[None, :])


def lane_tiles(count):
    return -(-count // 128)


def sounding_kernel(
    slots_each, jac_ref, got_ref, dev_ref, innov_ref, inv_ref, field_ref,
    dep_ref, out_ref, copy_ref, apart_ref, col_ref, tail_ref, grad_ref,
):
    at, steps = pl.program_id(0), pl.num_programs(0)
    step, count, width = jac_ref.shape
    devices, lanes = got_ref.shape[0], got_ref.shape[2]
    most = width // 128 * 128
    iota = lambda shape, axis: lax.broadcasted_iota(jnp.int32, shape, axis)
    copy_ref[...] = field_ref[...]

    @pl.when(at == 0)
    def _():
        apart_ref[...] = jnp.zeros_like(apart_ref)
        apart_ref[:, :slots_each, :] = got_ref[...].astype(jnp.float32)
        onehot = slots_of(dev_ref, dev_ref, 8, devices * 8)[0]
        onehot = jnp.where(onehot, 1.0, 0.0).astype(jnp.bfloat16)
        columns = matmul(onehot, apart_ref[...].reshape(devices * 8, lanes).astype(jnp.bfloat16))
        col_ref[...] = jnp.zeros_like(col_ref)
        col_ref[:count, :] = columns.astype(jnp.bfloat16)
        tail_ref[...] = columns[:, most:]
        grad_ref[...] = jnp.zeros_like(grad_ref)

    found = across(jac_ref[:, :, :most].reshape(step * count, most), col_ref[:, :most])
    square = (count, 128)
    mine = iota(square, 0) == iota(square, 1)
    weighted = []
    for k in range(step):
        channel = at * step + k
        observed = innov_ref[0, pl.ds(k, 1), :]
        own = jnp.where(mine, found[k * count:(k + 1) * count] - observed, 0.0)
        if width > most:
            tail = jac_ref[k, :, most:].astype(jnp.float32) * tail_ref[:, : width - most]
            own = own + jnp.concatenate([tail, jnp.zeros((count, 128 - (width - most)), jnp.float32)], axis=1)
        departure = jnp.sum(own, axis=1, keepdims=True)
        dep_ref[pl.ds(channel, 1), :] = jnp.sum(jnp.where(mine, departure, 0.0), axis=0, keepdims=True)[:, :count]
        weight = (departure * inv_ref[0, channel]).astype(jnp.bfloat16)
        weighted.append(weight.astype(jnp.float32))
    for group in range(0, count, 16):
        part = slice(group, group + 16)
        total = grad_ref[part, :width]
        for k in range(step):
            total = total + jac_ref[k, part, :].astype(jnp.float32) * weighted[k][part]
        grad_ref[part, :width] = total

    @pl.when(at == steps - 1)
    def _():
        slot = slots_of(dev_ref, dev_ref, 8, devices * 8)[2]
        onehot = jnp.where(iota((devices * 8, count), 0) == slot, 1.0, 0.0).astype(jnp.bfloat16)
        outgoing = matmul(onehot, grad_ref[...].astype(jnp.bfloat16))
        outgoing = outgoing.reshape(devices, 8, lanes)[:, :slots_each, :]
        out_ref[...] = outgoing.astype(out_ref.dtype)


def sounding_step(jacobian, got, col_dev, innovation, inv_error, field):
    count, channels, width = jacobian.shape
    devices, slots_each, lanes = got.shape
    step = next(n for n in (10, 8, 6, 5, 4, 3, 2, 1) if channels % n == 0)
    steps = channels // step
    block = -(-field.shape[0] // (8 * steps)) * 8
    innovation = jnp.pad(innovation.T, ((0, 0), (0, 128 - count))).reshape(steps, step, 128)
    whole = lambda shape: pl.BlockSpec(shape, lambda i: (0,) * len(shape))
    departures, grad, field = pl.pallas_call(
        functools.partial(sounding_kernel, slots_each),
        grid=(steps,),
        in_specs=[
            pl.BlockSpec((step, count, width), lambda i: (i, 0, 0)),
            whole(got.shape),
            whole((1, count)),
            pl.BlockSpec((1, step, 128), lambda i: (i, 0, 0)),
            pl.BlockSpec(memory_space=pltpu.SMEM),
            pl.BlockSpec((block, field.shape[1]), lambda i: (i, 0)),
        ],
        out_specs=[
            whole((channels, count)),
            whole(got.shape),
            pl.BlockSpec((block, field.shape[1]), lambda i: (i, 0)),
        ],
        out_shape=[
            jax.ShapeDtypeStruct((channels, count), jnp.float32),
            jax.ShapeDtypeStruct(got.shape, jnp.bfloat16),
            jax.ShapeDtypeStruct(field.shape, jnp.float32),
        ],
        scratch_shapes=[
            pltpu.VMEM((devices, 8, lanes), jnp.float32),
            pltpu.VMEM((128, lanes), jnp.bfloat16),
            pltpu.VMEM((count, 128), jnp.float32),
            pltpu.VMEM((count, lanes), jnp.float32),
        ],
        name="soundings",
    )(jnp.transpose(jacobian, (1, 0, 2)), got, col_dev.reshape(1, -1), innovation, inv_error[None, :], field)
    return departures.T, grad, field


def adjoint_kernel(
    lat, lon, lat_rows, cuts,
    give_ref, table_ref, std_ref, out_ref,
    arrived_ref, apart_ref, grads_ref, weight_ref,
    give_send, give_recv, swap_send, swap_recv, far_send, far_recv, lon_send, lon_recv,
):
    devices, slots_each, lanes = give_ref.shape
    slots = devices * slots_each
    rows, lon_cols = out_ref.shape
    log_lon = lon_cols.bit_length() - 1
    row, column = lax.axis_index("lat"), lax.axis_index("lon")
    me = row * lon + column
    odd = row % 2
    near = 1 - 2 * odd
    partner, step = row + near, 2 * near
    onward = jnp.logical_and(row + step >= 0, row + step < lat)
    comes = jnp.logical_and(row - step >= 0, row - step < lat)
    place = lambda other: (other // lon, other % lon)
    iota = lambda shape, axis: lax.broadcasted_iota(jnp.int32, shape, axis)
    chunks = range(len(cuts) - 1)
    part = [pl.ds(cuts[j], cuts[j + 1] - cuts[j]) for j in chunks]

    @pl.when(jnp.logical_not(comes))
    def _():
        grads_ref[2] = jnp.zeros_like(grads_ref[2])

    barrier = pltpu.get_barrier_semaphore()

    def greet(d, carry):
        pl.semaphore_signal(barrier, inc=1, device_id=place((me + d) % devices), device_id_type=MESH)
        return carry

    lax.fori_loop(1, devices, greet, 0)
    arrived_ref[me] = give_ref[me]
    apart_ref[...] = jnp.zeros_like(apart_ref)
    pl.semaphore_wait(barrier, devices - 1)

    def remote(source, target, send, recv, device):
        return pltpu.make_async_remote_copy(
            src_ref=source, dst_ref=target, send_sem=send, recv_sem=recv, device_id=device, device_id_type=MESH
        )

    for j in chunks:

        def give(d, carry):
            other = (me + d) % devices
            remote(
                give_ref.at[other, :, part[j]], arrived_ref.at[me, :, part[j]],
                give_send.at[j, other], give_recv.at[j, me], place(other),
            ).start()
            return carry

        lax.fori_loop(1, devices, give, 0)

    total = 9 * slots
    flat = (1, total)
    at = iota(flat, 1).astype(jnp.float32)
    block = jnp.floor((at + 0.5) / slots)
    within = at - block * slots
    source = jnp.floor((within + 0.5) / slots_each)
    order = within - source * slots_each
    up = jnp.floor((block + 0.5) / 3.0)
    along = block - 3.0 * up
    lat_shift = jnp.where(up == 0.0, 0.0, jnp.where(up == 1.0, 1.0, -1.0)) * near.astype(jnp.float32)
    lon_shift = jnp.where(along == 0.0, 0.0, jnp.where(along == 1.0, -1.0, 1.0))
    owner_row = jnp.clip(row.astype(jnp.float32) + lat_shift, 0.0, lat - 1.0)
    owner_col = column.astype(jnp.float32) + lon_shift
    owner_col = jnp.where(owner_col < 0.0, owner_col + lon, jnp.where(owner_col >= lon, owner_col - lon, owner_col))
    wanted = ((owner_row * lon + owner_col) * slots_each + order).astype(jnp.int32)
    listed = table_ref[...].reshape(devices, table_ref.shape[2])
    chosen = jnp.where(iota((listed.shape[1], total), 0) == wanted, 1.0, 0.0).astype(jnp.bfloat16)
    mine = iota((devices, total), 0) == source.astype(jnp.int32)

    def position(values):
        found = matmul(values.astype(jnp.bfloat16), chosen)
        return jnp.sum(jnp.where(mine, found, 0.0), axis=0, keepdims=True)

    slot_row = position(listed >> log_lon) + lat_shift * lat_rows
    slot_col = position(listed & (lon_cols - 1)) + lon_shift * lon_cols
    down = iota((lon_cols, total), 0).astype(jnp.float32)
    col_weight = tap_value(slot_col - down, lon_cols // 2)
    for i in range(0, lat_rows, 2):
        for k in range(2):
            value = col_weight * tap_value(slot_row - (i + k), LHALF)
            high, low = halves(value)
            weight_ref[i // 2, k * lon_cols:(k + 1) * lon_cols, :] = high
            weight_ref[i // 2, (k + 2) * lon_cols:(k + 3) * lon_cols, :] = low

    padded = iota((slots, devices * 8), 1)
    compact = jnp.logical_and(
        iota((slots, devices * 8), 0) == (padded >> 3) * slots_each + (padded & 7), (padded & 7) < slots_each
    )
    compact = jnp.where(compact, 1.0, 0.0).astype(jnp.bfloat16)

    def receive(j):
        def wait(d, carry):
            other = (me + d) % devices
            copy = remote(
                give_ref.at[other, :, part[j]], arrived_ref.at[other, :, part[j]],
                give_send.at[j, other], give_recv.at[j, other], place(other),
            )
            copy.wait_send()
            copy.wait_recv()
            return carry

        lax.fori_loop(1, devices, wait, 0)
        apart_ref[:, :slots_each, part[j]] = arrived_ref[:, :, part[j]].astype(jnp.float32)
        wide = apart_ref[:, :, part[j]].reshape(devices * 8, cuts[j + 1] - cuts[j]).astype(jnp.bfloat16)
        grads_ref[0, 0, :, part[j]] = matmul(compact, wide).astype(jnp.bfloat16)

    def swap(j, b):
        return remote(
            grads_ref.at[0, b, :, part[j]], grads_ref.at[1, b, :, part[j]],
            swap_send.at[j, b], swap_recv.at[j, b], (partner, column),
        )

    def forward(j, b):
        return remote(
            grads_ref.at[1, b, :, part[j]], grads_ref.at[2, b, :, part[j]],
            far_send.at[j, b], far_recv.at[j, b], (row + step, column),
        )

    def to_right(j, a):
        return remote(
            grads_ref.at[a, 0, :, part[j]], grads_ref.at[a, 1, :, part[j]],
            lon_send.at[0, j, a], lon_recv.at[0, j, a], (row, (column + 1) % lon),
        )

    def to_left(j, a):
        return remote(
            grads_ref.at[a, 0, :, part[j]], grads_ref.at[a, 2, :, part[j]],
            lon_send.at[1, j, a], lon_recv.at[1, j, a], (row, (column + lon - 1) % lon),
        )

    def send_lon(j, a):
        to_right(j, a).start()
        to_left(j, a).start()

    def await_lon(j, a):
        to_right(j, a).wait_recv()
        to_left(j, a).wait_recv()

    def pass_on(j, b):
        swap(j, b).wait_recv()

        @pl.when(onward)
        def _():
            forward(j, b).start()

    def await_far(j, b):
        @pl.when(comes)
        def _():
            forward(j, b).wait_recv()

    def compute(j):
        count = cuts[j + 1] - cuts[j]
        kept = min(count, rows // lat_rows - cuts[j])
        grads = grads_ref[:, :, :, part[j]].reshape(total, count)

        def two(i, carry):
            result = matmul(weight_ref[i], grads)
            result = (result[: 2 * lon_cols] + result[2 * lon_cols:]) * std_ref[:, part[j]]
            for k in range(2):
                piece = result[k * lon_cols:(k + 1) * lon_cols].T
                out_ref[pl.ds(cuts[j] * lat_rows + 2 * i + k, kept, stride=lat_rows), :] = piece[:kept]
            return carry

        lax.fori_loop(0, lat_rows // 2, two, 0)

    lon_first, lat_first = chunks[:1], chunks[1:]
    for j in lon_first:
        receive(j)
        send_lon(j, 0)
    for j in lat_first:
        receive(j)
        swap(j, 0).start()
    for j in lon_first:
        swap(j, 0).start()
        await_lon(j, 0)
        swap(j, 1).start()
        swap(j, 2).start()
    for j in lat_first:
        pass_on(j, 0)
        send_lon(j, 0)
        send_lon(j, 1)
    for j in lon_first:
        pass_on(j, 0)
    for j in lat_first:
        await_far(j, 0)
        send_lon(j, 2)
    for b in (1, 2):
        for j in lon_first:
            pass_on(j, b)
    for b in range(3):
        for j in lon_first:
            await_far(j, b)
    for j in lon_first:
        compute(j)
    for j in lat_first:
        for a in range(3):
            await_lon(j, a)
        compute(j)
    for j in chunks:
        for b in range(3) if j in lon_first else (0,):
            swap(j, b).wait_send()

            @pl.when(onward)
            def _():
                forward(j, b).wait_send()

        for a in (0,) if j in lon_first else range(3):
            to_right(j, a).wait_send()
            to_left(j, a).wait_send()


def adjoint_step(outgoing, table, std_dev, lat_rows, lon_cols):
    lat, lon = lax.axis_size("lat"), lax.axis_size("lon")
    devices, slots_each, lanes = outgoing.shape
    slots, width = devices * slots_each, std_dev.shape[0]
    cuts = [*range(0, width // 256 * 256 + 1, 256), lanes]
    pieces = len(cuts) - 1
    std_dev = jnp.pad(std_dev, (0, lanes - width))[None, :]
    vmem = pl.BlockSpec(memory_space=pltpu.VMEM)
    dma = pltpu.SemaphoreType.DMA
    bf16, f32 = jnp.bfloat16, jnp.float32
    return pl.pallas_call(
        functools.partial(adjoint_kernel, lat, lon, lat_rows, cuts),
        in_specs=[vmem] * 3,
        out_specs=vmem,
        out_shape=jax.ShapeDtypeStruct((width * lat_rows, lon_cols), f32),
        scratch_shapes=[
            pltpu.VMEM((devices, slots_each, lanes), bf16),
            pltpu.VMEM((devices, 8, lanes), f32),
            pltpu.VMEM((3, 3, slots, lanes), bf16),
            pltpu.VMEM((lat_rows // 2, 4 * lon_cols, 9 * slots), bf16),
            *[dma((pieces, devices))] * 2,
            *[dma((pieces, 3))] * 4,
            *[dma((2, pieces, 3))] * 2,
        ],
        compiler_params=pltpu.CompilerParams(collective_id=1, has_side_effects=True),
        name="adjoint",
    )(outgoing, table, std_dev)


def local(control, std_dev, col_dev, col_cell, jacobian, innovation, inv_error):
    width, lat_rows, lon_cols = control.shape
    devices = lax.axis_size("lat") * lax.axis_size("lon")
    slots_each = max(2, 2 * col_cell.shape[0] // devices)
    increment, table, got = dense_step(control, col_dev, col_cell, std_dev, slots_each)
    departures, outgoing, increment = sounding_step(jacobian, got, col_dev, innovation, inv_error, increment)
    adjoint = adjoint_step(outgoing, table, std_dev, lat_rows, lon_cols)
    return departures, increment.reshape(control.shape), adjoint.reshape(control.shape)


def solution(mesh):
    placed = (
        P(None, "lat", "lon"),
        P(),
        P(("lat", "lon"), None),
        P(("lat", "lon")),
        P(("lat", "lon"), None, None),
        P(("lat", "lon"), None),
        P(),
    )
    return jax.shard_map(
        local,
        mesh=mesh,
        in_specs=placed,
        out_specs=(P(("lat", "lon"), None), P(None, "lat", "lon"), P(None, "lat", "lon")),
        check_vma=False,
    )
```

time: 161 us -> 117 us (0.73); the launches traced: 158 us -> 116 us
  waiting for transfers between devices: 29.9 us -> 0 us
  Pallas kernels: 91.2 us -> 108 us
  local copies, waits for them, and re-layouts: 19.6 us -> 7.24 us
  starting transfers between devices: 9.86 us -> 0 us
  other arithmetic: 4.13 us -> 0 us
  between operations: 2.33 us -> 0.65 us
    pallas_call x2, Pallas kernels: 27.8 us -> 60.3 us  [the longest x1 42.1 us: adjoint_step(): pl.pallas_call(functools.partial(adjoint_kernel, lat, lon, lat_rows, cuts...]
    ppermute x4 -> x0, waiting for transfers between devices: 20.6 us -> none  [around(): return (lax.ppermute(array, axis, up), lax.ppermute(array, axis, down))]
    pallas_call x1, Pallas kernels: 63.4 us -> 48 us  [dense_step(): pl.pallas_call(functools.partial(dense_kernel, lat, lon, lat_rows, slots_...]
    all_to_all x1 -> x0, waiting for transfers between devices: 9.28 us -> none  [local(): lax.all_to_all(outgoing.reshape(devices, slots_each, wide), ('lat', 'lon'...]
    ppermute x4 -> x0, starting transfers between devices: 6.59 us -> none  [around(): return (lax.ppermute(array, axis, up), lax.ppermute(array, axis, down))]
    unnamed x24 -> x1, local copies, waits for them, and re-layouts: 7.1 us -> 3.14 us
    all_to_all x1 -> x0, starting transfers between devices: 3.27 us -> none  [local(): lax.all_to_all(outgoing.reshape(devices, slots_each, wide), ('lat', 'lon'...]
    reshape x4 -> x1, local copies, waits for them, and re-layouts: 3.53 us -> 0.65 us  [sounding_step(): jnp.pad(innovation.T, ((0, 0), (0, 128 - count))).reshape(steps, step, 128)]
  transfers between devices with their start and end apart: 5 -> 0, of which waited for: 5 -> 0; matrix products, arithmetic and copies ran while one was open for 4% -> 0% of each run, Pallas kernels for 0% -> 0%
where the time goes in v2:
time: 117 us; the launch traced here: 116 us
  Pallas kernels  108 us (92%)
  local copies, waits for them, and re-layouts  7.24 us (6%)
    pallas_call x1, Pallas kernels, dense_step(): pl.pallas_call(functools.partial(dense_kernel, lat, lon, lat_rows, slots_...  48 us
    pallas_call x1, Pallas kernels, adjoint_step(): pl.pallas_call(functools.partial(adjoint_kernel, lat, lon, lat_rows, cuts...  42.1 us
    pallas_call x1, Pallas kernels, sounding_step(): pl.pallas_call(functools.partial(sounding_kernel, slots_each), grid=(step...  18.2 us
    unnamed x1, local copies, waits for them, and re-layouts  3.14 us

profile of v2, /device:TPU:2, one launch (start us, length us, event | category | flops | bytes accessed | tf_op | source)
XLA Modules:
  0.0 116.2 jit_solution(16346959077145610363)
XLA Ops:
  0.6 1.3 %broadcast_in_dim.13.std_ref = f32[1,548]{1,0:T(1,128)} reshape(f32[548]{0:T(1024)} %param.8) | data formatting | bytes 4384 | tf_op jit(solution)/shard_map/broadcast_in_dim | solution.py:491
  1.9 0.7 pad.9
  2.6 0.6 broadcast_in_dim.15.std_ref
  3.2 0.9 pad.8
  4.1 0.7 reshape.24.innov_ref
  4.7 48.0 %dense.1 = (f32[4384,128]{1,0:T(8,128)}, s32[32,1,256]{2,1,0:T(1,128)}, bf16[32,6,640]{2,1,0:T(8,128)(2,1)}) custom-call(f32[4384,128]{1,0:T(8,128)} %bitcast.11, s32[1,96]{1,0:T(1,128)} %bitcast.13, s32[1,96]{1,0:T(1,128)} %bitcast.16, f32[1,548]{1,0:T(1,128)} %broadcast_in_dim.13.std_ref), custom_call_target="tpu_custom_call" | custom-call | tf_op jit(solution)/shard_map/dense/pallas_call | solution.py:459
  52.7 18.2 %soundings.1 = (f32[150,96]{1,0:T(8,128)}, bf16[32,6,640]{2,1,0:T(8,128)(2,1)}, f32[4384,128]{1,0:T(8,128)}) custom-call(bf16[150,96,548]{2,1,0:T(8,128)(2,1)} %bitcast.9, bf16[32,6,640]{2,1,0:T(8,128)(2,1)} %get-tuple-element.9.got_ref, s32[1,96]{1,0:T(1,128)} %bitcast.14, f32[15,10,128]{2,1,0:T(8,128)} %reshape.24.innov_ref, f32[1,150]{1,0:T(1,128)} %bitcast.15, ...), custom_call_target="tpu_custom_call" | custom-call | tf_op jit(solution)/shard_map/soundings/pallas_call | solution.py:560
  70.9 42.1 %adjoint.1 = f32[4384,128]{1,0:T(8,128)} custom-call(bf16[32,6,640]{2,1,0:T(8,128)(2,1)} %get-tuple-element.13.give_ref, s32[32,1,256]{2,1,0:T(1,128)} %get-tuple-element.14.table_ref, f32[1,640]{1,0:T(1,128)} %broadcast_in_dim.15.std_ref), custom_call_target="tpu_custom_call" | custom-call | tf_op jit(solution)/shard_map/adjoint/pallas_call | solution.py:817
  113.0 3.1 %copy.11 = f32[548,8,128]{2,1,0:T(8,128)} copy(f32[548,8,128]{2,1,0:T(8,128)} %bitcast.10) | data formatting | bytes 4489216

commit v3 on v2

--- a/solution.py
+++ b/solution.py
@@ -234,7 +234,7 @@
 
     def spread(c, carry):
         std_row_ref[pl.ds(pl.multiple_of(c * lat_rows, lat_rows), lat_rows), :] = jnp.full(
-            (lat_rows, lon_cols), std_ref[0, c], jnp.float32
+            (lat_rows, lon_cols), std_ref[c], jnp.float32
         )
         return carry
 
@@ -488,114 +488,155 @@
         ],
         compiler_params=pltpu.CompilerParams(collective_id=0, has_side_effects=True),
         name="dense",
-    )(control.reshape(rows, lon_cols), col_dev.reshape(1, -1), col_cell[None, :], std_dev[None, :])
+    )(control.reshape(rows, lon_cols), col_dev.reshape(1, -1), col_cell[None, :], std_dev)
 
 
 def lane_tiles(count):
     return -(-count // 128)
 
 
+PIECE = 16
+
+
+def piece_slot(index, slots_each, piece, kind):
+    device, row = index >> 4, index & (PIECE - 1)
+    spare = PIECE - 2 * slots_each
+    if kind < 2:
+        number = row - kind * slots_each
+        valid = jnp.logical_and(number >= 0, number < slots_each)
+    else:
+        number = row - 2 * slots_each + piece * spare
+        valid = jnp.logical_and(row >= 2 * slots_each, number < slots_each)
+    return jnp.where(valid, device * 8 + number, -1)
+
+
 def sounding_kernel(
-    slots_each, jac_ref, got_ref, dev_ref, innov_ref, inv_ref, field_ref,
-    dep_ref, out_ref, copy_ref, apart_ref, col_ref, tail_ref, grad_ref,
+    slots_each, step,
+    jac_hbm, got_ref, dev_ref, innov_ref, inv_ref, field_hbm,
+    dep_ref, out_ref, copy_hbm,
+    jac_ref, field_ref, apart_ref, col_ref, tail_ref, weight_ref, grad_ref, jac_sem, field_sem,
 ):
-    at, steps = pl.program_id(0), pl.num_programs(0)
-    step, count, width = jac_ref.shape
+    channels, count, width = jac_ref.shape
+    steps = channels // step
     devices, lanes = got_ref.shape[0], got_ref.shape[2]
     most = width // 128 * 128
     iota = lambda shape, axis: lax.broadcasted_iota(jnp.int32, shape, axis)
-    copy_ref[...] = field_ref[...]
-
-    @pl.when(at == 0)
-    def _():
-        apart_ref[...] = jnp.zeros_like(apart_ref)
-        apart_ref[:, :slots_each, :] = got_ref[...].astype(jnp.float32)
-        onehot = slots_of(dev_ref, dev_ref, 8, devices * 8)[0]
-        onehot = jnp.where(onehot, 1.0, 0.0).astype(jnp.bfloat16)
-        columns = matmul(onehot, apart_ref[...].reshape(devices * 8, lanes).astype(jnp.bfloat16))
-        col_ref[...] = jnp.zeros_like(col_ref)
-        col_ref[:count, :] = columns.astype(jnp.bfloat16)
-        tail_ref[...] = columns[:, most:]
-        grad_ref[...] = jnp.zeros_like(grad_ref)
-
-    found = across(jac_ref[:, :, :most].reshape(step * count, most), col_ref[:, :most])
-    square = (count, 128)
-    mine = iota(square, 0) == iota(square, 1)
-    weighted = []
-    for k in range(step):
-        channel = at * step + k
-        observed = innov_ref[0, pl.ds(k, 1), :]
-        own = jnp.where(mine, found[k * count:(k + 1) * count] - observed, 0.0)
-        if width > most:
-            tail = jac_ref[k, :, most:].astype(jnp.float32) * tail_ref[:, : width - most]
-            own = own + jnp.concatenate([tail, jnp.zeros((count, 128 - (width - most)), jnp.float32)], axis=1)
-        departure = jnp.sum(own, axis=1, keepdims=True)
-        dep_ref[pl.ds(channel, 1), :] = jnp.sum(jnp.where(mine, departure, 0.0), axis=0, keepdims=True)[:, :count]
-        weight = (departure * inv_ref[0, channel]).astype(jnp.bfloat16)
-        weighted.append(weight.astype(jnp.float32))
-    for group in range(0, count, 16):
-        part = slice(group, group + 16)
-        total = grad_ref[part, :width]
+
+    def load(b):
+        part = pl.ds(b * step, step)
+        return pltpu.make_async_copy(jac_hbm.at[part], jac_ref.at[part], jac_sem.at[b])
+
+    take = pltpu.make_async_copy(field_hbm, field_ref, field_sem.at[0])
+    leave = pltpu.make_async_copy(field_ref, copy_hbm, field_sem.at[1])
+    load(0).start()
+    take.start()
+
+    def begin(b, carry):
+        load(b).start()
+        return carry
+
+    lax.fori_loop(1, steps, begin, 0)
+    apart_ref[...] = jnp.zeros_like(apart_ref)
+    apart_ref[:, :slots_each, :] = got_ref[...].astype(jnp.float32)
+    onehot, _, slot = slots_of(dev_ref, dev_ref, 8, devices * 8)
+    onehot = jnp.where(onehot, 1.0, 0.0).astype(jnp.bfloat16)
+    columns = matmul(onehot, apart_ref[...].reshape(devices * 8, lanes).astype(jnp.bfloat16))
+    col_ref[...] = columns.astype(jnp.bfloat16)
+    tail_ref[...] = columns[:, most:]
+    grad_ref[...] = jnp.zeros_like(grad_ref)
+    square = (count, count)
+
+    def product(b):
+        block = jac_ref[pl.ds(b * step, step), :, :most]
+        return across(block.reshape(step * count, most), col_ref[:, :most])
+
+    def depart(b, found):
+        mine = iota(square, 0) == iota(square, 1)
         for k in range(step):
-            total = total + jac_ref[k, part, :].astype(jnp.float32) * weighted[k][part]
-        grad_ref[part, :width] = total
-
-    @pl.when(at == steps - 1)
-    def _():
-        slot = slots_of(dev_ref, dev_ref, 8, devices * 8)[2]
-        onehot = jnp.where(iota((devices * 8, count), 0) == slot, 1.0, 0.0).astype(jnp.bfloat16)
-        outgoing = matmul(onehot, grad_ref[...].astype(jnp.bfloat16))
-        outgoing = outgoing.reshape(devices, 8, lanes)[:, :slots_each, :]
-        out_ref[...] = outgoing.astype(out_ref.dtype)
+            channel = b * step + k
+            own = jnp.where(mine, found[k * count:(k + 1) * count] - innov_ref[pl.ds(channel, 1), :], 0.0)
+            if width > most:
+                tail = jac_ref[channel, :, most:].astype(jnp.float32) * tail_ref[:, : width - most]
+                own = own + jnp.concatenate([tail, jnp.zeros((count, count - (width - most)), jnp.float32)], axis=1)
+            departure = jnp.sum(own, axis=1, keepdims=True)
+            dep_ref[pl.ds(channel, 1), :] = jnp.sum(jnp.where(mine, departure, 0.0), axis=0, keepdims=True)
+            weight = (departure * inv_ref[channel]).astype(jnp.bfloat16).astype(jnp.float32)
+            weight_ref[k] = jnp.broadcast_to(weight, (count, 128))
+
+    def gradient(b):
+        for group in range(0, count, 16):
+            part = slice(group, group + 16)
+            for lane in range(0, width, 128):
+                end = min(lane + 128, width)
+                total = grad_ref[part, lane:end]
+                for k in range(step):
+                    values = jac_ref[b * step + k, part, lane:end].astype(jnp.float32)
+                    total = total + values * weight_ref[k, part, : end - lane]
+                grad_ref[part, lane:end] = total
+
+    load(0).wait()
+    depart(0, product(0))
+    take.wait()
+    leave.start()
+
+    def body(b, carry):
+        load(b).wait()
+        found = product(b)
+        gradient(b - 1)
+        depart(b, found)
+        return carry
+
+    lax.fori_loop(1, steps, body, 0)
+    gradient(steps - 1)
+    grads = grad_ref[...].astype(jnp.bfloat16)
+    for piece in range(2):
+        packed = jnp.zeros((devices * PIECE, 128), jnp.float32)
+        for kind in range(3):
+            held = piece_slot(iota((devices * PIECE, count), 0), slots_each, piece, kind)
+            onehot = jnp.where(held == slot, 1.0, 0.0).astype(jnp.bfloat16)
+            tile = (2 * piece + kind if kind < 2 else 4) * 128
+            packed = packed + matmul(onehot, grads[:, tile:tile + 128])
+        out_ref[piece] = packed.astype(out_ref.dtype)
+    leave.wait()
 
 
 def sounding_step(jacobian, got, col_dev, innovation, inv_error, field):
     count, channels, width = jacobian.shape
     devices, slots_each, lanes = got.shape
     step = next(n for n in (10, 8, 6, 5, 4, 3, 2, 1) if channels % n == 0)
-    steps = channels // step
-    block = -(-field.shape[0] // (8 * steps)) * 8
-    innovation = jnp.pad(innovation.T, ((0, 0), (0, 128 - count))).reshape(steps, step, 128)
-    whole = lambda shape: pl.BlockSpec(shape, lambda i: (0,) * len(shape))
+    vmem, hbm = pl.BlockSpec(memory_space=pltpu.VMEM), pl.BlockSpec(memory_space=pl.ANY)
     departures, grad, field = pl.pallas_call(
-        functools.partial(sounding_kernel, slots_each),
-        grid=(steps,),
-        in_specs=[
-            pl.BlockSpec((step, count, width), lambda i: (i, 0, 0)),
-            whole(got.shape),
-            whole((1, count)),
-            pl.BlockSpec((1, step, 128), lambda i: (i, 0, 0)),
-            pl.BlockSpec(memory_space=pltpu.SMEM),
-            pl.BlockSpec((block, field.shape[1]), lambda i: (i, 0)),
-        ],
-        out_specs=[
-            whole((channels, count)),
-            whole(got.shape),
-            pl.BlockSpec((block, field.shape[1]), lambda i: (i, 0)),
-        ],
+        functools.partial(sounding_kernel, slots_each, step),
+        in_specs=[hbm, vmem, vmem, vmem, pl.BlockSpec(memory_space=pltpu.SMEM), hbm],
+        out_specs=[vmem, vmem, hbm],
         out_shape=[
             jax.ShapeDtypeStruct((channels, count), jnp.float32),
-            jax.ShapeDtypeStruct(got.shape, jnp.bfloat16),
+            jax.ShapeDtypeStruct((2, devices * PIECE, 128), jnp.bfloat16),
             jax.ShapeDtypeStruct(field.shape, jnp.float32),
         ],
         scratch_shapes=[
+            pltpu.VMEM((channels, count, width), jnp.bfloat16),
+            pltpu.VMEM(field.shape, jnp.float32),
             pltpu.VMEM((devices, 8, lanes), jnp.float32),
-            pltpu.VMEM((128, lanes), jnp.bfloat16),
+            pltpu.VMEM((count, lanes), jnp.bfloat16),
             pltpu.VMEM((count, 128), jnp.float32),
+            pltpu.VMEM((step, count, 128), jnp.float32),
             pltpu.VMEM((count, lanes), jnp.float32),
+            pltpu.SemaphoreType.DMA((channels // step,)),
+            pltpu.SemaphoreType.DMA((2,)),
         ],
         name="soundings",
-    )(jnp.transpose(jacobian, (1, 0, 2)), got, col_dev.reshape(1, -1), innovation, inv_error[None, :], field)
+    )(jnp.transpose(jacobian, (1, 0, 2)), got, col_dev.reshape(1, -1), innovation.T, inv_error, field)
     return departures.T, grad, field
 
 
 def adjoint_kernel(
-    lat, lon, lat_rows, cuts,
+    lat, lon, lat_rows, slots_each, cuts,
     give_ref, table_ref, std_ref, out_ref,
-    arrived_ref, apart_ref, grads_ref, weight_ref,
+    arrived_ref, compact_ref, grads_ref, weight_ref,
     give_send, give_recv, swap_send, swap_recv, far_send, far_recv, lon_send, lon_recv,
 ):
-    devices, slots_each, lanes = give_ref.shape
+    devices = lat * lon
     slots = devices * slots_each
     rows, lon_cols = out_ref.shape
     log_lon = lon_cols.bit_length() - 1
@@ -622,8 +663,11 @@
         return carry
 
     lax.fori_loop(1, devices, greet, 0)
-    arrived_ref[me] = give_ref[me]
-    apart_ref[...] = jnp.zeros_like(apart_ref)
+
+    def piece_of(d):
+        return pl.ds(pl.multiple_of(d * PIECE, PIECE), PIECE)
+
+    arrived_ref[:, piece_of(me), :] = give_ref[:, piece_of(me), :]
     pl.semaphore_wait(barrier, devices - 1)
 
     def remote(source, target, send, recv, device):
@@ -631,14 +675,16 @@
             src_ref=source, dst_ref=target, send_sem=send, recv_sem=recv, device_id=device, device_id_type=MESH
         )
 
-    for j in chunks:
+    def hand(j, other, source):
+        return remote(
+            give_ref.at[j, piece_of(other)], arrived_ref.at[j, piece_of(source)],
+            give_send.at[j, other], give_recv.at[j, source], place(other),
+        )
+
+    for j in range(2):
 
         def give(d, carry):
-            other = (me + d) % devices
-            remote(
-                give_ref.at[other, :, part[j]], arrived_ref.at[me, :, part[j]],
-                give_send.at[j, other], give_recv.at[j, me], place(other),
-            ).start()
+            hand(j, (me + d) % devices, me).start()
             return carry
 
         lax.fori_loop(1, devices, give, 0)
@@ -677,27 +723,27 @@
             weight_ref[i // 2, k * lon_cols:(k + 1) * lon_cols, :] = high
             weight_ref[i // 2, (k + 2) * lon_cols:(k + 3) * lon_cols, :] = low
 
-    padded = iota((slots, devices * 8), 1)
-    compact = jnp.logical_and(
-        iota((slots, devices * 8), 0) == (padded >> 3) * slots_each + (padded & 7), (padded & 7) < slots_each
-    )
-    compact = jnp.where(compact, 1.0, 0.0).astype(jnp.bfloat16)
+    spread = (slots, devices * PIECE)
+    for at, (piece, kind) in enumerate(((0, 0), (0, 1), (0, 2), (1, 2))):
+        held = piece_slot(iota(spread, 1), slots_each, piece, kind)
+        wanted = jnp.where(held < 0, -1, (held >> 3) * slots_each + (held & 7))
+        compact_ref[at] = jnp.where(wanted == iota(spread, 0), 1.0, 0.0).astype(jnp.bfloat16)
 
     def receive(j):
         def wait(d, carry):
             other = (me + d) % devices
-            copy = remote(
-                give_ref.at[other, :, part[j]], arrived_ref.at[other, :, part[j]],
-                give_send.at[j, other], give_recv.at[j, other], place(other),
-            )
-            copy.wait_send()
-            copy.wait_recv()
+            hand(j, other, other).wait_send()
+            hand(j, other, other).wait_recv()
             return carry
 
         lax.fori_loop(1, devices, wait, 0)
-        apart_ref[:, :slots_each, part[j]] = arrived_ref[:, :, part[j]].astype(jnp.float32)
-        wide = apart_ref[:, :, part[j]].reshape(devices * 8, cuts[j + 1] - cuts[j]).astype(jnp.bfloat16)
-        grads_ref[0, 0, :, part[j]] = matmul(compact, wide).astype(jnp.bfloat16)
+        for kind in range(2):
+            tile = (2 * j + kind) * 128
+            grads_ref[0, 0, :, tile:tile + 128] = matmul(compact_ref[kind], arrived_ref[j]).astype(jnp.bfloat16)
+
+    def receive_rest():
+        rest = matmul(compact_ref[2], arrived_ref[0]) + matmul(compact_ref[3], arrived_ref[1])
+        grads_ref[0, 0, :, part[2]] = rest.astype(jnp.bfloat16)
 
     def swap(j, b):
         return remote(
@@ -758,38 +804,38 @@
 
         lax.fori_loop(0, lat_rows // 2, two, 0)
 
-    lon_first, lat_first = chunks[:1], chunks[1:]
+    lon_first = (0, 2)
+    receive(0)
+    send_lon(0, 0)
+    swap(0, 0).start()
+    receive(1)
+    swap(1, 0).start()
+    receive_rest()
+    send_lon(2, 0)
+    swap(2, 0).start()
+    pass_on(0, 0)
+    await_lon(0, 0)
+    swap(0, 1).start()
+    swap(0, 2).start()
+    pass_on(1, 0)
+    send_lon(1, 0)
+    send_lon(1, 1)
+    pass_on(2, 0)
+    await_lon(2, 0)
+    swap(2, 1).start()
+    swap(2, 2).start()
+    await_far(1, 0)
+    send_lon(1, 2)
     for j in lon_first:
-        receive(j)
-        send_lon(j, 0)
-    for j in lat_first:
-        receive(j)
-        swap(j, 0).start()
-    for j in lon_first:
-        swap(j, 0).start()
-        await_lon(j, 0)
-        swap(j, 1).start()
-        swap(j, 2).start()
-    for j in lat_first:
-        pass_on(j, 0)
-        send_lon(j, 0)
-        send_lon(j, 1)
-    for j in lon_first:
-        pass_on(j, 0)
-    for j in lat_first:
-        await_far(j, 0)
-        send_lon(j, 2)
-    for b in (1, 2):
-        for j in lon_first:
-            pass_on(j, b)
-    for b in range(3):
-        for j in lon_first:
-            await_far(j, b)
-    for j in lon_first:
-        compute(j)
-    for j in lat_first:
-        for a in range(3):
-            await_lon(j, a)
+        pass_on(j, 1)
+        pass_on(j, 2)
+    for j in chunks:
+        if j in lon_first:
+            for b in range(3):
+                await_far(j, b)
+        else:
+            for a in range(3):
+                await_lon(j, a)
         compute(j)
     for j in chunks:
         for b in range(3) if j in lon_first else (0,):
@@ -804,27 +850,28 @@
             to_left(j, a).wait_send()
 
 
-def adjoint_step(outgoing, table, std_dev, lat_rows, lon_cols):
+def adjoint_step(outgoing, table, std_dev, slots_each, lat_rows, lon_cols):
     lat, lon = lax.axis_size("lat"), lax.axis_size("lon")
-    devices, slots_each, lanes = outgoing.shape
+    devices = lat * lon
     slots, width = devices * slots_each, std_dev.shape[0]
-    cuts = [*range(0, width // 256 * 256 + 1, 256), lanes]
+    lanes = lane_tiles(width) * 128
+    cuts = [0, 256, 512, lanes]
     pieces = len(cuts) - 1
     std_dev = jnp.pad(std_dev, (0, lanes - width))[None, :]
     vmem = pl.BlockSpec(memory_space=pltpu.VMEM)
     dma = pltpu.SemaphoreType.DMA
     bf16, f32 = jnp.bfloat16, jnp.float32
     return pl.pallas_call(
-        functools.partial(adjoint_kernel, lat, lon, lat_rows, cuts),
+        functools.partial(adjoint_kernel, lat, lon, lat_rows, slots_each, cuts),
         in_specs=[vmem] * 3,
         out_specs=vmem,
         out_shape=jax.ShapeDtypeStruct((width * lat_rows, lon_cols), f32),
         scratch_shapes=[
-            pltpu.VMEM((devices, slots_each, lanes), bf16),
-            pltpu.VMEM((devices, 8, lanes), f32),
+            pltpu.VMEM((2, devices * PIECE, 128), bf16),
+            pltpu.VMEM((4, slots, devices * PIECE), bf16),
             pltpu.VMEM((3, 3, slots, lanes), bf16),
             pltpu.VMEM((lat_rows // 2, 4 * lon_cols, 9 * slots), bf16),
-            *[dma((pieces, devices))] * 2,
+            *[dma((2, devices))] * 2,
             *[dma((pieces, 3))] * 4,
             *[dma((2, pieces, 3))] * 2,
         ],
@@ -839,7 +886,7 @@
     slots_each = max(2, 2 * col_cell.shape[0] // devices)
     increment, table, got = dense_step(control, col_dev, col_cell, std_dev, slots_each)
     departures, outgoing, increment = sounding_step(jacobian, got, col_dev, innovation, inv_error, increment)
-    adjoint = adjoint_step(outgoing, table, std_dev, lat_rows, lon_cols)
+    adjoint = adjoint_step(outgoing, table, std_dev, slots_each, lat_rows, lon_cols)
     return departures, increment.reshape(control.shape), adjoint.reshape(control.shape)
 
 

time: 117 us -> 107 us (0.915)
  Pallas kernels: 108 us -> 102 us
  local copies, waits for them, and re-layouts: 7.24 us -> 4.42 us
    pallas_call x2, Pallas kernels: 60.3 us -> 54 us  [the longest x1 40.3 us: adjoint_step(): pl.pallas_call(functools.partial(adjoint_kernel, lat, lon, lat_rows, slot...]
    broadcast_in_dim x1 -> x0, local copies, waits for them, and re-layouts: 1.27 us -> none  [dense_step(): std_dev[None, :]]
where the time goes in v3:
time: 107 us
  Pallas kernels  102 us (95%)
  local copies, waits for them, and re-layouts  4.42 us (4%)
    pallas_call x1, Pallas kernels, dense_step(): pl.pallas_call(functools.partial(dense_kernel, lat, lon, lat_rows, slots_...  47.9 us
    pallas_call x1, Pallas kernels, adjoint_step(): pl.pallas_call(functools.partial(adjoint_kernel, lat, lon, lat_rows, slot...  40.3 us
    pallas_call x1, Pallas kernels, sounding_step(): pl.pallas_call(functools.partial(sounding_kernel, slots_each, step), in_s...  13.7 us
    unnamed x1, local copies, waits for them, and re-layouts  3.14 us

profile of v3, /device:TPU:2, one launch (start us, length us, event | category | flops | bytes accessed | tf_op | source)
XLA Modules:
  0.0 107.0 jit_solution(14149790423145412168)
XLA Ops:
  0.6 0.7 pad.4
  1.3 0.6 broadcast_in_dim.7.std_ref
  1.9 47.9 %dense.1 = (f32[4384,128]{1,0:T(8,128)}, s32[32,1,256]{2,1,0:T(1,128)}, bf16[32,6,640]{2,1,0:T(8,128)(2,1)}) custom-call(f32[4384,128]{1,0:T(8,128)} %bitcast.10, s32[1,96]{1,0:T(1,128)} %bitcast.12, s32[1,96]{1,0:T(1,128)} %bitcast.14, f32[548]{0:T(1024)} %std_ref.1), custom_call_target="tpu_custom_call" | custom-call | tf_op jit(solution)/shard_map/dense/pallas_call | solution.py:459
  49.9 13.7 %soundings.1 = (f32[150,96]{1,0:T(8,128)}, bf16[2,512,128]{2,1,0:T(8,128)(2,1)}, f32[4384,128]{1,0:T(8,128)}) custom-call(bf16[150,96,548]{2,1,0:T(8,128)(2,1)} %bitcast.8, bf16[32,6,640]{2,1,0:T(8,128)(2,1)} %get-tuple-element.9.got_ref, s32[1,96]{1,0:T(1,128)} %bitcast.13, f32[150,96]{1,0:T(8,128)} %bitcast.11, f32[150]{0:T(256)} %inv_ref.1, ...), custom_call_target="tpu_custom_call" | custom-call | tf_op jit(solution)/shard_map/soundings/pallas_call | solution.py:608
  63.6 40.3 %adjoint.1 = f32[4384,128]{1,0:T(8,128)} custom-call(bf16[2,512,128]{2,1,0:T(8,128)(2,1)} %get-tuple-element.13.give_ref, s32[32,1,256]{2,1,0:T(1,128)} %get-tuple-element.14.table_ref, f32[1,640]{1,0:T(1,128)} %broadcast_in_dim.7.std_ref), custom_call_target="tpu_custom_call" | custom-call | tf_op jit(solution)/shard_map/adjoint/pallas_call | solution.py:864
  103.9 3.1 %copy.11 = f32[548,8,128]{2,1,0:T(8,128)} copy(f32[548,8,128]{2,1,0:T(8,128)} %bitcast.9) | data formatting | bytes 4489216

commit v4 on v3

--- a/solution.py
+++ b/solution.py
@@ -10,6 +10,8 @@
 
 LHALF = 8
 MESH = pl.DeviceIdType.MESH
+VMEM = 48 << 20
+DENSE_VMEM = 64300000
 
 
 def tap_weights(offset, half_width):
@@ -63,12 +65,12 @@
 
 def dense_kernel(
     lat, lon, lat_rows, slots_each,
-    ctrl_hbm, dev_ref, ask_ref, std_ref,
-    inc_hbm, table_ref, got_ref,
-    ctrl_ref, inc_ref, wanted_ref, own_ref, swap_ref, far_ref, g_ref, to_right_ref, to_left_ref, from_left_ref, from_right_ref,
+    ctrl_hbm, dev_hbm, ask_hbm, std_hbm,
+    inc_ref, table_ref, got_ref,
+    ctrl_ref, dev_ref, ask_ref, std_ref, wanted_ref, own_ref, swap_ref, far_ref, g_ref, to_right_ref, to_left_ref, from_left_ref, from_right_ref,
     band_ref, mid_ref, edge_ref, std_row_ref, cell_ref, row_ref, pick_ref,
     swap_send, swap_recv, far_send, far_recv, lon_send, lon_recv,
-    want_send, want_recv, col_send, col_recv, load_sem, store_sem,
+    want_send, want_recv, col_send, col_recv, load_sem, small_sem,
 ):
     rows, lon_cols = ctrl_ref.shape
     width = rows // lat_rows
@@ -139,15 +141,20 @@
     def load(k, part):
         return pltpu.make_async_copy(ctrl_hbm.at[part], ctrl_ref.at[part], load_sem.at[k])
 
-    def store(k, part):
-        return pltpu.make_async_copy(inc_ref.at[part], inc_hbm.at[part], store_sem.at[k])
-
     def begin(k, carry):
         load(k, chunk_of(k)).start()
         return carry
 
+    small = [
+        pltpu.make_async_copy(source, target, small_sem.at[at])
+        for at, (source, target) in enumerate(((dev_hbm, dev_ref), (ask_hbm, ask_ref), (std_hbm, std_ref)))
+    ]
+    for copy in small:
+        copy.start()
     lax.fori_loop(0, full, begin, 0)
     load(full, last).start()
+    for copy in small:
+        copy.wait()
     onehot, cell_at, _ = slots_of(dev_ref, ask_ref, slots_each, wanted_ref.shape[2])
     wanted_ref[0] = jnp.sum(jnp.where(onehot, cell_at, 0.0), axis=0, keepdims=True).astype(jnp.int32)
 
@@ -379,7 +386,6 @@
         def _():
             await_lon(done, half_of(done))
             lon_last(done)
-            store(done, chunk_of(done)).start()
 
         @pl.when(jnp.logical_and(behind >= 0, behind < early))
         def _():
@@ -389,7 +395,6 @@
         def _():
             await_far(behind, chunk_of(behind))
             lat_last(behind)
-            store(behind, chunk_of(behind)).start()
 
         def give(group):
             pick(pl.multiple_of(group * 2 * CHUNK, 2 * CHUNK), 2 * CHUNK, group)
@@ -407,7 +412,6 @@
         def _():
             await_far(full, last)
             lat_rest()
-            store(full, last).start()
             pick(full * CHUNK, rest, full // 2)
             send_back(full // 2)
 
@@ -423,7 +427,6 @@
         def _():
             forward(k, part).wait_send()
 
-        store(k, part).wait()
         to_right(k, half).wait_send()
         to_left(k, half).wait_send()
 
@@ -453,13 +456,13 @@
     pieces = rows // CHUNK + 1
     lanes = lane_tiles(width) * lon_cols
     listed = (1, lane_tiles(devices * slots_each) * 128)
-    vmem, hbm = pl.BlockSpec(memory_space=pltpu.VMEM), pl.BlockSpec(memory_space=pl.ANY)
+    vmem, hbm = pl.BlockSpec(memory_space=pltpu.VMEM), pl.BlockSpec(memory_space=pltpu.HBM)
     dma = pltpu.SemaphoreType.DMA
     bf16, f32 = jnp.bfloat16, jnp.float32
     return pl.pallas_call(
         functools.partial(dense_kernel, lat, lon, lat_rows, slots_each),
-        in_specs=[hbm, vmem, vmem, pl.BlockSpec(memory_space=pltpu.SMEM)],
-        out_specs=[hbm, vmem, vmem],
+        in_specs=[hbm] * 4,
+        out_specs=[vmem, vmem, vmem],
         out_shape=[
             jax.ShapeDtypeStruct((rows, lon_cols), f32),
             jax.ShapeDtypeStruct((devices, *listed), jnp.int32),
@@ -467,7 +470,9 @@
         ],
         scratch_shapes=[
             pltpu.VMEM((rows, lon_cols), f32),
-            pltpu.VMEM((rows, lon_cols), f32),
+            pltpu.VMEM((1, col_cell.shape[0]), jnp.int32),
+            pltpu.VMEM((1, col_cell.shape[0]), jnp.int32),
+            pltpu.SMEM(std_dev.shape, f32),
             pltpu.VMEM((1, *listed), jnp.int32),
             pltpu.VMEM((rows, lon_cols), bf16),
             pltpu.VMEM((rows, lon_cols), bf16),
@@ -484,9 +489,10 @@
             *[dma((pieces,))] * 4,
             *[dma((2, pieces))] * 2,
             *[dma((devices,))] * 4,
-            *[dma((pieces,))] * 2,
+            dma((pieces,)),
+            dma((3,)),
         ],
-        compiler_params=pltpu.CompilerParams(collective_id=0, has_side_effects=True),
+        compiler_params=pltpu.CompilerParams(collective_id=0, has_side_effects=True, vmem_limit_bytes=DENSE_VMEM),
         name="dense",
     )(control.reshape(rows, lon_cols), col_dev.reshape(1, -1), col_cell[None, :], std_dev)
 
@@ -510,11 +516,10 @@
     return jnp.where(valid, device * 8 + number, -1)
 
 
-def sounding_kernel(
+def sounding_part(
     slots_each, step,
-    jac_hbm, got_ref, dev_ref, innov_ref, inv_ref, field_hbm,
-    dep_ref, out_ref, copy_hbm,
-    jac_ref, field_ref, apart_ref, col_ref, tail_ref, weight_ref, grad_ref, jac_sem, field_sem,
+    jac_hbm, got_ref, dev_ref, innov_ref, inv_ref, dep_ref, out_ref,
+    jac_ref, apart_ref, col_ref, tail_ref, weight_ref, grad_ref, jac_sem,
 ):
     channels, count, width = jac_ref.shape
     steps = channels // step
@@ -526,16 +531,11 @@
         part = pl.ds(b * step, step)
         return pltpu.make_async_copy(jac_hbm.at[part], jac_ref.at[part], jac_sem.at[b])
 
-    take = pltpu.make_async_copy(field_hbm, field_ref, field_sem.at[0])
-    leave = pltpu.make_async_copy(field_ref, copy_hbm, field_sem.at[1])
-    load(0).start()
-    take.start()
-
     def begin(b, carry):
         load(b).start()
         return carry
 
-    lax.fori_loop(1, steps, begin, 0)
+    lax.fori_loop(0, steps, begin, 0)
     apart_ref[...] = jnp.zeros_like(apart_ref)
     apart_ref[:, :slots_each, :] = got_ref[...].astype(jnp.float32)
     onehot, _, slot = slots_of(dev_ref, dev_ref, 8, devices * 8)
@@ -576,8 +576,6 @@
 
     load(0).wait()
     depart(0, product(0))
-    take.wait()
-    leave.start()
 
     def body(b, carry):
         load(b).wait()
@@ -597,43 +595,14 @@
             tile = (2 * piece + kind if kind < 2 else 4) * 128
             packed = packed + matmul(onehot, grads[:, tile:tile + 128])
         out_ref[piece] = packed.astype(out_ref.dtype)
-    leave.wait()
-
-
-def sounding_step(jacobian, got, col_dev, innovation, inv_error, field):
-    count, channels, width = jacobian.shape
-    devices, slots_each, lanes = got.shape
-    step = next(n for n in (10, 8, 6, 5, 4, 3, 2, 1) if channels % n == 0)
-    vmem, hbm = pl.BlockSpec(memory_space=pltpu.VMEM), pl.BlockSpec(memory_space=pl.ANY)
-    departures, grad, field = pl.pallas_call(
-        functools.partial(sounding_kernel, slots_each, step),
-        in_specs=[hbm, vmem, vmem, vmem, pl.BlockSpec(memory_space=pltpu.SMEM), hbm],
-        out_specs=[vmem, vmem, hbm],
-        out_shape=[
-            jax.ShapeDtypeStruct((channels, count), jnp.float32),
-            jax.ShapeDtypeStruct((2, devices * PIECE, 128), jnp.bfloat16),
-            jax.ShapeDtypeStruct(field.shape, jnp.float32),
-        ],
-        scratch_shapes=[
-            pltpu.VMEM((channels, count, width), jnp.bfloat16),
-            pltpu.VMEM(field.shape, jnp.float32),
-            pltpu.VMEM((devices, 8, lanes), jnp.float32),
-            pltpu.VMEM((count, lanes), jnp.bfloat16),
-            pltpu.VMEM((count, 128), jnp.float32),
-            pltpu.VMEM((step, count, 128), jnp.float32),
-            pltpu.VMEM((count, lanes), jnp.float32),
-            pltpu.SemaphoreType.DMA((channels // step,)),
-            pltpu.SemaphoreType.DMA((2,)),
-        ],
-        name="soundings",
-    )(jnp.transpose(jacobian, (1, 0, 2)), got, col_dev.reshape(1, -1), innovation.T, inv_error, field)
-    return departures.T, grad, field
 
 
 def adjoint_kernel(
-    lat, lon, lat_rows, slots_each, cuts,
-    give_ref, table_ref, std_ref, out_ref,
-    arrived_ref, compact_ref, grads_ref, weight_ref,
+    lat, lon, lat_rows, slots_each, cuts, step,
+    jac_hbm, got_ref, dev_ref, innov_ref, inv_ref, table_ref, std_ref,
+    dep_ref, out_ref,
+    jac_ref, apart_ref, col_ref, tail_ref, scale_ref, grad_ref, jac_sem,
+    give_ref, arrived_ref, compact_ref, grads_ref, weight_ref, std_row_ref,
     give_send, give_recv, swap_send, swap_recv, far_send, far_recv, lon_send, lon_recv,
 ):
     devices = lat * lon
@@ -644,9 +613,9 @@
     me = row * lon + column
     odd = row % 2
     near = 1 - 2 * odd
-    partner, step = row + near, 2 * near
-    onward = jnp.logical_and(row + step >= 0, row + step < lat)
-    comes = jnp.logical_and(row - step >= 0, row - step < lat)
+    partner, stride = row + near, 2 * near
+    onward = jnp.logical_and(row + stride >= 0, row + stride < lat)
+    comes = jnp.logical_and(row - stride >= 0, row - stride < lat)
     place = lambda other: (other // lon, other % lon)
     iota = lambda shape, axis: lax.broadcasted_iota(jnp.int32, shape, axis)
     chunks = range(len(cuts) - 1)
@@ -663,6 +632,12 @@
         return carry
 
     lax.fori_loop(1, devices, greet, 0)
+    sounding_part(
+        slots_each, step, jac_hbm, got_ref, dev_ref, innov_ref, inv_ref, dep_ref, give_ref,
+        jac_ref, apart_ref, col_ref, tail_ref, scale_ref, grad_ref, jac_sem,
+    )
+    std_row_ref[...] = jnp.zeros_like(std_row_ref)
+    std_row_ref[:, : std_ref.shape[0]] = std_ref[...].reshape(1, -1)
 
     def piece_of(d):
         return pl.ds(pl.multiple_of(d * PIECE, PIECE), PIECE)
@@ -754,7 +729,7 @@
     def forward(j, b):
         return remote(
             grads_ref.at[1, b, :, part[j]], grads_ref.at[2, b, :, part[j]],
-            far_send.at[j, b], far_recv.at[j, b], (row + step, column),
+            far_send.at[j, b], far_recv.at[j, b], (row + stride, column),
         )
 
     def to_right(j, a):
@@ -796,7 +771,7 @@
 
         def two(i, carry):
             result = matmul(weight_ref[i], grads)
-            result = (result[: 2 * lon_cols] + result[2 * lon_cols:]) * std_ref[:, part[j]]
+            result = (result[: 2 * lon_cols] + result[2 * lon_cols:]) * std_row_ref[:, part[j]]
             for k in range(2):
                 piece = result[k * lon_cols:(k + 1) * lon_cols].T
                 out_ref[pl.ds(cuts[j] * lat_rows + 2 * i + k, kept, stride=lat_rows), :] = piece[:kept]
@@ -850,34 +825,47 @@
             to_left(j, a).wait_send()
 
 
-def adjoint_step(outgoing, table, std_dev, slots_each, lat_rows, lon_cols):
+def analysis_step(jacobian, got, table, col_dev, innovation, inv_error, std_dev, lat_rows, lon_cols):
     lat, lon = lax.axis_size("lat"), lax.axis_size("lon")
-    devices = lat * lon
-    slots, width = devices * slots_each, std_dev.shape[0]
-    lanes = lane_tiles(width) * 128
+    count, channels, width = jacobian.shape
+    devices, slots_each, lanes = got.shape
+    slots, rows = devices * slots_each, width * lat_rows
     cuts = [0, 256, 512, lanes]
     pieces = len(cuts) - 1
-    std_dev = jnp.pad(std_dev, (0, lanes - width))[None, :]
-    vmem = pl.BlockSpec(memory_space=pltpu.VMEM)
+    step = next(n for n in (10, 8, 6, 5, 4, 3, 2, 1) if channels % n == 0)
+    vmem, hbm = pl.BlockSpec(memory_space=pltpu.VMEM), pl.BlockSpec(memory_space=pl.ANY)
     dma = pltpu.SemaphoreType.DMA
     bf16, f32 = jnp.bfloat16, jnp.float32
-    return pl.pallas_call(
-        functools.partial(adjoint_kernel, lat, lon, lat_rows, slots_each, cuts),
-        in_specs=[vmem] * 3,
-        out_specs=vmem,
-        out_shape=jax.ShapeDtypeStruct((width * lat_rows, lon_cols), f32),
+    departures, adjoint = pl.pallas_call(
+        functools.partial(adjoint_kernel, lat, lon, lat_rows, slots_each, cuts, step),
+        in_specs=[hbm, vmem, vmem, vmem, pl.BlockSpec(memory_space=pltpu.SMEM), vmem, vmem],
+        out_specs=[vmem, vmem],
+        out_shape=[
+            jax.ShapeDtypeStruct((channels, count), f32),
+            jax.ShapeDtypeStruct((rows, lon_cols), f32),
+        ],
         scratch_shapes=[
+            pltpu.VMEM((channels, count, width), bf16),
+            pltpu.VMEM((devices, 8, lanes), f32),
+            pltpu.VMEM((count, lanes), bf16),
+            pltpu.VMEM((count, 128), f32),
+            pltpu.VMEM((step, count, 128), f32),
+            pltpu.VMEM((count, lanes), f32),
+            dma((channels // step,)),
+            pltpu.VMEM((2, devices * PIECE, 128), bf16),
             pltpu.VMEM((2, devices * PIECE, 128), bf16),
             pltpu.VMEM((4, slots, devices * PIECE), bf16),
             pltpu.VMEM((3, 3, slots, lanes), bf16),
             pltpu.VMEM((lat_rows // 2, 4 * lon_cols, 9 * slots), bf16),
+            pltpu.VMEM((1, lanes), f32),
             *[dma((2, devices))] * 2,
             *[dma((pieces, 3))] * 4,
             *[dma((2, pieces, 3))] * 2,
         ],
-        compiler_params=pltpu.CompilerParams(collective_id=1, has_side_effects=True),
-        name="adjoint",
-    )(outgoing, table, std_dev)
+        compiler_params=pltpu.CompilerParams(collective_id=1, has_side_effects=True, vmem_limit_bytes=VMEM),
+        name="analysis",
+    )(jnp.transpose(jacobian, (1, 0, 2)), got, col_dev.reshape(1, -1), innovation.T, inv_error, table, std_dev)
+    return departures, adjoint
 
 
 def local(control, std_dev, col_dev, col_cell, jacobian, innovation, inv_error):
@@ -885,9 +873,10 @@
     devices = lax.axis_size("lat") * lax.axis_size("lon")
     slots_each = max(2, 2 * col_cell.shape[0] // devices)
     increment, table, got = dense_step(control, col_dev, col_cell, std_dev, slots_each)
-    departures, outgoing, increment = sounding_step(jacobian, got, col_dev, innovation, inv_error, increment)
-    adjoint = adjoint_step(outgoing, table, std_dev, slots_each, lat_rows, lon_cols)
-    return departures, increment.reshape(control.shape), adjoint.reshape(control.shape)
+    departures, adjoint = analysis_step(
+        jacobian, got, table, col_dev, innovation, inv_error, std_dev, lat_rows, lon_cols
+    )
+    return departures.T, increment.reshape(control.shape), adjoint.reshape(control.shape)
 
 
 def solution(mesh):

time: 107 us -> 102 us (0.953)
  Pallas kernels: 102 us -> 95.3 us
    pallas_call x2 -> x1, Pallas kernels: 54 us -> 47.4 us  [analysis_step(): pl.pallas_call(functools.partial(adjoint_kernel, lat, lon, lat_rows, slot...]
    unnamed x1 -> x17, local copies, waits for them, and re-layouts: 3.14 us -> 5.11 us
where the time goes in v4:
time: 102 us; the launch traced here: 101 us
  Pallas kernels  95.3 us (93%)
  local copies, waits for them, and re-layouts  5.11 us (5%)
    pallas_call x1, Pallas kernels, dense_step(): pl.pallas_call(functools.partial(dense_kernel, lat, lon, lat_rows, slots_...  47.9 us
    pallas_call x1, Pallas kernels, analysis_step(): pl.pallas_call(functools.partial(adjoint_kernel, lat, lon, lat_rows, slot...  47.4 us
    unnamed x17, local copies, waits for them, and re-layouts  5.11 us

profile of v4, /device:TPU:2, one launch (start us, length us, event | category | flops | bytes accessed | tf_op | source)
XLA Modules:
  0.0 101.1 jit_solution(13389090228154591121)
XLA Ops:
  0.6 0.0 copy-start.3
  0.6 0.0 copy-start.5
  0.7 0.0 copy-start.1
  0.7 0.0 copy-start.4
  0.7 47.9 %dense.1 = (f32[4384,128]{1,0:T(8,128)}, s32[32,1,256]{2,1,0:T(1,128)}, bf16[32,6,640]{2,1,0:T(8,128)(2,1)}) custom-call(f32[4384,128]{1,0:T(8,128)} %bitcast.14, s32[1,96]{1,0:T(1,128)} %bitcast.11, s32[1,96]{1,0:T(1,128)} %bitcast.16, f32[548]{0:T(1024)} %std_ref.1), custom_call_target="tpu_custom_call" | custom-call | tf_op jit(solution)/shard_map/dense/pallas_call | solution.py:462
  48.6 0.0 copy-done.3
  48.6 0.0 copy-done.5
  48.6 0.0 copy-done.1
  48.6 0.0 copy-done.4
  48.6 0.0 copy-start
  48.6 1.0 copy-done
  49.6 0.0 copy-start.2
  49.6 0.8 copy-done.2
  50.3 0.0 copy-start.6
  50.3 47.4 %analysis.1 = (f32[150,96]{1,0:T(8,128)S(1)}, f32[4384,128]{1,0:T(8,128)S(1)}) custom-call(bf16[150,96,548]{2,1,0:T(8,128)(2,1)} %bitcast.13, bf16[32,6,640]{2,1,0:T(8,128)(2,1)S(1)} %copy-done, s32[1,96]{1,0:T(1,128)S(1)} %bitcast.12, f32[150,96]{1,0:T(8,128)S(1)} %bitcast.9, f32[150]{0:T(256)S(1)} %copy-done.5, s32[32,1,256]{2,1,0:T(1,128)S(1)} %copy-done.2, ...), custom_call_target="tpu_custom_call" | custom-call | tf_op jit(solution)/shard_map/analysis/pallas_call | solution.py:839
  97.7 0.6 copy.13
  98.4 0.0 copy-done.6
  98.4 1.4 %copy.14 = f32[548,8,128]{2,1,0:T(8,128)} copy(f32[548,8,128]{2,1,0:T(8,128)S(1)} %bitcast.15) | data formatting | bytes 4489216
  99.7 1.4 %copy.15 = f32[548,8,128]{2,1,0:T(8,128)} copy(f32[548,8,128]{2,1,0:T(8,128)S(1)} %bitcast.8) | data formatting | bytes 4489216
Async XLA Ops:
  0.6 47.9 %copy-start.3 = (f32[548]{0:T(1024)S(1)}, f32[548]{0:T(1024)}, u32[]{:S(2)}) copy-start(f32[548]{0:T(1024)} %std_ref.1) | copy-start | bytes 6580
  0.6 47.9 %copy-start.5 = (f32[150]{0:T(256)S(1)}, f32[150]{0:T(256)}, u32[]{:S(2)}) copy-start(f32[150]{0:T(256)} %inv_ref.1) | copy-start | bytes 1804
  0.7 47.9 %copy-start.1 = (f32[96,150]{0,1:T(8,128)S(1)}, f32[96,150]{0,1:T(8,128)}, u32[]{:S(2)}) copy-start(f32[96,150]{0,1:T(8,128)} %param.12) | copy-start | bytes 172804
  0.7 47.9 %copy-start.4 = (s32[96,1]{0,1:T(1,128)S(1)}, s32[96,1]{0,1:T(1,128)}, u32[]{:S(2)}) copy-start(s32[96,1]{0,1:T(1,128)} %param.9) | copy-start | bytes 1156
  48.6 1.0 copy-start
  49.6 0.8 copy-start.2
  50.3 48.0 %copy-start.6 = (f32[4384,128]{1,0:T(8,128)S(1)}, f32[4384,128]{1,0:T(8,128)}, u32[]{:S(2)}) copy-start(f32[4384,128]{1,0:T(8,128)} %get-tuple-element.11) | copy-start | bytes 6733828

commit v5 on v4

--- a/solution.py
+++ b/solution.py
@@ -70,7 +70,7 @@
     ctrl_ref, dev_ref, ask_ref, std_ref, wanted_ref, own_ref, swap_ref, far_ref, g_ref, to_right_ref, to_left_ref, from_left_ref, from_right_ref,
     band_ref, mid_ref, edge_ref, std_row_ref, cell_ref, row_ref, pick_ref,
     swap_send, swap_recv, far_send, far_recv, lon_send, lon_recv,
-    want_send, want_recv, col_send, col_recv, load_sem, small_sem,
+    want_send, want_recv, col_send, col_recv, load_sem, small_sem, token_sem,
 ):
     rows, lon_cols = ctrl_ref.shape
     width = rows // lat_rows
@@ -89,11 +89,15 @@
 
     barrier = pltpu.get_barrier_semaphore()
 
-    def greet(d, carry):
-        pl.semaphore_signal(barrier, inc=1, device_id=place((me + d) % devices), device_id_type=MESH)
-        return carry
-
-    lax.fori_loop(1, devices, greet, 0)
+    right, left = (row, (column + 1) % lon), (row, (column + lon - 1) % lon)
+
+    def tell(semaphore, device):
+        pl.semaphore_signal(semaphore, inc=1, device_id=device, device_id_type=MESH)
+
+    for d in range(1, lat):
+        tell(barrier, ((row + d) % lat, column))
+    tell(barrier, right)
+    tell(barrier, left)
 
     def chunk_of(k):
         return pl.ds(pl.multiple_of(k * CHUNK, CHUNK), CHUNK)
@@ -164,13 +168,18 @@
 
     load(0, chunk_of(0)).wait()
     round_own(chunk_of(0))
-    pl.semaphore_wait(barrier, devices - 1)
+    pl.semaphore_wait(barrier, lat + 1)
+
+    def pass_tokens():
+        tell(token_sem.at[0], right)
+        tell(token_sem.at[1], left)
+
+    pass_tokens()
 
     def ask(d, carry):
         request(me, (me + d) % devices, me, (me + d) % devices).start()
         return carry
 
-    lax.fori_loop(1, devices, ask, 0)
 
     def send_own(k, carry):
         load(k + 1, chunk_of(k + 1)).wait()
@@ -247,21 +256,6 @@
 
     lax.fori_loop(0, width, spread, 0)
 
-    def hear(d, carry):
-        other = (me + d) % devices
-        asked = request(other, other, other, other)
-        asked.wait_send()
-        asked.wait_recv()
-        return carry
-
-    lax.fori_loop(1, devices, hear, 0)
-    listed = jnp.broadcast_to(table_ref[...].astype(jnp.float32), (devices, 8, table_ref.shape[2]))
-    wants = iota(listed.shape, 2) == iota(listed.shape, 1) + me * slots_each
-    cell = jnp.sum(jnp.where(wants, listed, 0.0), axis=2, keepdims=True).astype(jnp.int32)
-    cell = jnp.broadcast_to(cell, (devices, 8, lon_cols)).reshape(devices * 8, lon_cols)
-    row_ref[...] = cell >> log_lon
-    cell_ref[...] = jnp.where((cell & (lon_cols - 1)) == iota(cell.shape, 1), 1.0, 0.0).astype(jnp.bfloat16)
-
     def lat_product(ref, first, second):
         def pair(ref):
             return jnp.concatenate([ref[first, :], ref[second, :]], axis=1)
@@ -338,6 +332,25 @@
 
         lax.fori_loop(1, devices, give, 0)
 
+    def learn():
+        def hear(d, carry):
+            other = (me + d) % devices
+            asked = request(other, other, other, other)
+            asked.wait_send()
+            asked.wait_recv()
+            return carry
+
+        lax.fori_loop(1, devices, hear, 0)
+        listed = jnp.broadcast_to(table_ref[...].astype(jnp.float32), (devices, 8, table_ref.shape[2]))
+        wants = iota(listed.shape, 2) == iota(listed.shape, 1) + me * slots_each
+        cell = jnp.sum(jnp.where(wants, listed, 0.0), axis=2, keepdims=True).astype(jnp.int32)
+        cell = jnp.broadcast_to(cell, (devices, 8, lon_cols)).reshape(devices * 8, lon_cols)
+        row_ref[...] = cell >> log_lon
+        cell_ref[...] = jnp.where((cell & (lon_cols - 1)) == iota(cell.shape, 1), 1.0, 0.0).astype(jnp.bfloat16)
+
+    each = -(-(lon // 2) // 4)
+    rounds = -(-(lon // 2) // each)
+
     def stage(k, carry):
         def arrive(k, part):
             swap(k, part).wait_recv()
@@ -359,6 +372,24 @@
         def _():
             arrive(full, last)
 
+        @pl.when(k < rounds)
+        def _():
+            def step(n, carry):
+                pl.semaphore_wait(token_sem.at[0], 1)
+                pl.semaphore_wait(token_sem.at[1], 1)
+
+                @pl.when(k * each + n + 1 < rounds * each)
+                def _():
+                    pass_tokens()
+
+                return carry
+
+            lax.fori_loop(0, each, step, 0)
+
+        @pl.when(k == rounds - 1)
+        def _():
+            lax.fori_loop(1, devices, ask, 0)
+
         def await_lon(k, part):
             to_right(k, part).wait_recv()
             to_left(k, part).wait_recv()
@@ -395,6 +426,10 @@
         def _():
             await_far(behind, chunk_of(behind))
             lat_last(behind)
+
+        @pl.when(k == 5)
+        def _():
+            learn()
 
         def give(group):
             pick(pl.multiple_of(group * 2 * CHUNK, 2 * CHUNK), 2 * CHUNK, group)
@@ -491,6 +526,7 @@
             *[dma((devices,))] * 4,
             dma((pieces,)),
             dma((3,)),
+            pltpu.SemaphoreType.REGULAR((2,)),
         ],
         compiler_params=pltpu.CompilerParams(collective_id=0, has_side_effects=True, vmem_limit_bytes=DENSE_VMEM),
         name="dense",

time: 102 us -> 101 us (level)
  no operation moved by 1% of the time
where the time goes in v5:
time: 101 us
  Pallas kernels  95 us (94%)
  local copies, waits for them, and re-layouts  5.11 us (5%)
    pallas_call x1, Pallas kernels, dense_step(): pl.pallas_call(functools.partial(dense_kernel, lat, lon, lat_rows, slots_...  48.5 us
    pallas_call x1, Pallas kernels, analysis_step(): pl.pallas_call(functools.partial(adjoint_kernel, lat, lon, lat_rows, slot...  46.5 us
    unnamed x17, local copies, waits for them, and re-layouts  5.11 us

profile of v5, /device:TPU:2, one launch (start us, length us, event | category | flops | bytes accessed | tf_op | source)
XLA Modules:
  0.0 100.8 jit_solution(16066721657750843012)
XLA Ops:
  0.6 0.0 copy-start.3
  0.6 0.0 copy-start.5
  0.7 0.0 copy-start.1
  0.7 0.0 copy-start.4
  0.7 48.5 %dense.1 = (f32[4384,128]{1,0:T(8,128)}, s32[32,1,256]{2,1,0:T(1,128)}, bf16[32,6,640]{2,1,0:T(8,128)(2,1)}) custom-call(f32[4384,128]{1,0:T(8,128)} %bitcast.14, s32[1,96]{1,0:T(1,128)} %bitcast.11, s32[1,96]{1,0:T(1,128)} %bitcast.16, f32[548]{0:T(1024)} %std_ref.1), custom_call_target="tpu_custom_call" | custom-call | tf_op jit(solution)/shard_map/dense/pallas_call | solution.py:497
  49.2 0.0 copy-done.3
  49.2 0.0 copy-done.5
  49.2 0.0 copy-done.1
  49.2 0.0 copy-done.4
  49.3 0.0 copy-start
  49.3 1.0 copy-done
  50.2 0.0 copy-start.2
  50.2 0.8 copy-done.2
  51.0 0.0 copy-start.6
  51.0 46.5 %analysis.1 = (f32[150,96]{1,0:T(8,128)S(1)}, f32[4384,128]{1,0:T(8,128)S(1)}) custom-call(bf16[150,96,548]{2,1,0:T(8,128)(2,1)} %bitcast.13, bf16[32,6,640]{2,1,0:T(8,128)(2,1)S(1)} %copy-done, s32[1,96]{1,0:T(1,128)S(1)} %bitcast.12, f32[150,96]{1,0:T(8,128)S(1)} %bitcast.9, f32[150]{0:T(256)S(1)} %copy-done.5, s32[32,1,256]{2,1,0:T(1,128)S(1)} %copy-done.2, ...), custom_call_target="tpu_custom_call" | custom-call | tf_op jit(solution)/shard_map/analysis/pallas_call | solution.py:875
  97.4 0.6 copy.13
  98.1 0.0 copy-done.6
  98.1 1.4 %copy.14 = f32[548,8,128]{2,1,0:T(8,128)} copy(f32[548,8,128]{2,1,0:T(8,128)S(1)} %bitcast.15) | data formatting | bytes 4489216
  99.5 1.4 %copy.15 = f32[548,8,128]{2,1,0:T(8,128)} copy(f32[548,8,128]{2,1,0:T(8,128)S(1)} %bitcast.8) | data formatting | bytes 4489216
Async XLA Ops:
  0.6 48.6 %copy-start.3 = (f32[548]{0:T(1024)S(1)}, f32[548]{0:T(1024)}, u32[]{:S(2)}) copy-start(f32[548]{0:T(1024)} %std_ref.1) | copy-start | bytes 6580
  0.6 48.6 %copy-start.5 = (f32[150]{0:T(256)S(1)}, f32[150]{0:T(256)}, u32[]{:S(2)}) copy-start(f32[150]{0:T(256)} %inv_ref.1) | copy-start | bytes 1804
  0.7 48.6 %copy-start.1 = (f32[96,150]{0,1:T(8,128)S(1)}, f32[96,150]{0,1:T(8,128)}, u32[]{:S(2)}) copy-start(f32[96,150]{0,1:T(8,128)} %param.12) | copy-start | bytes 172804
  0.7 48.6 %copy-start.4 = (s32[96,1]{0,1:T(1,128)S(1)}, s32[96,1]{0,1:T(1,128)}, u32[]{:S(2)}) copy-start(s32[96,1]{0,1:T(1,128)} %param.9) | copy-start | bytes 1156
  49.3 1.0 copy-start
  50.2 0.8 copy-start.2
  51.0 47.1 %copy-start.6 = (f32[4384,128]{1,0:T(8,128)S(1)}, f32[4384,128]{1,0:T(8,128)}, u32[]{:S(2)}) copy-start(f32[4384,128]{1,0:T(8,128)} %get-tuple-element.11) | copy-start | bytes 6733828

commit v6 on v5

--- a/solution.py
+++ b/solution.py
@@ -75,7 +75,7 @@
     rows, lon_cols = ctrl_ref.shape
     width = rows // lat_rows
     full, rest = rows // CHUNK, rows % CHUNK
-    early = full // 4 * 2
+    early = 2
     log_lat, log_lon = lat_rows.bit_length() - 1, lon_cols.bit_length() - 1
     lon_half = lon_cols // 2
     row, column = lax.axis_index("lat"), lax.axis_index("lon")

time: 101 us -> 100 us (0.990)
  Pallas kernels: 95 us -> 93.2 us
    pallas_call x1, Pallas kernels: 48.5 us -> 47.2 us  [dense_step(): pl.pallas_call(functools.partial(dense_kernel, lat, lon, lat_rows, slots_...]
where the time goes in v6:
time: 100 us; the launch traced here: 99.1 us
  Pallas kernels  93.2 us (93%)
  local copies, waits for them, and re-layouts  5.11 us (5%)
    pallas_call x1, Pallas kernels, dense_step(): pl.pallas_call(functools.partial(dense_kernel, lat, lon, lat_rows, slots_...  47.2 us
    pallas_call x1, Pallas kernels, analysis_step(): pl.pallas_call(functools.partial(adjoint_kernel, lat, lon, lat_rows, slot...  46 us
    unnamed x17, local copies, waits for them, and re-layouts  5.11 us

profile of v6, /device:TPU:2, one launch (start us, length us, event | category | flops | bytes accessed | tf_op | source)
XLA Modules:
  0.0 99.1 jit_solution(8012695612660769394)
XLA Ops:
  0.6 0.0 copy-start.3
  0.6 0.0 copy-start.5
  0.7 0.0 copy-start.1
  0.7 0.0 copy-start.4
  0.7 47.2 %dense.1 = (f32[4384,128]{1,0:T(8,128)}, s32[32,1,256]{2,1,0:T(1,128)}, bf16[32,6,640]{2,1,0:T(8,128)(2,1)}) custom-call(f32[4384,128]{1,0:T(8,128)} %bitcast.14, s32[1,96]{1,0:T(1,128)} %bitcast.11, s32[1,96]{1,0:T(1,128)} %bitcast.16, f32[548]{0:T(1024)} %std_ref.1), custom_call_target="tpu_custom_call" | custom-call | tf_op jit(solution)/shard_map/dense/pallas_call | solution.py:497
  47.9 0.0 copy-done.3
  47.9 0.0 copy-done.5
  47.9 0.0 copy-done.1
  47.9 0.0 copy-done.4
  47.9 0.0 copy-start
  47.9 1.0 copy-done
  48.9 0.0 copy-start.2
  48.9 0.8 copy-done.2
  49.6 0.0 copy-start.6
  49.6 46.0 %analysis.1 = (f32[150,96]{1,0:T(8,128)S(1)}, f32[4384,128]{1,0:T(8,128)S(1)}) custom-call(bf16[150,96,548]{2,1,0:T(8,128)(2,1)} %bitcast.13, bf16[32,6,640]{2,1,0:T(8,128)(2,1)S(1)} %copy-done, s32[1,96]{1,0:T(1,128)S(1)} %bitcast.12, f32[150,96]{1,0:T(8,128)S(1)} %bitcast.9, f32[150]{0:T(256)S(1)} %copy-done.5, s32[32,1,256]{2,1,0:T(1,128)S(1)} %copy-done.2, ...), custom_call_target="tpu_custom_call" | custom-call | tf_op jit(solution)/shard_map/analysis/pallas_call | solution.py:875
  95.7 0.6 copy.13
  96.3 0.0 copy-done.6
  96.3 1.4 %copy.14 = f32[548,8,128]{2,1,0:T(8,128)} copy(f32[548,8,128]{2,1,0:T(8,128)S(1)} %bitcast.15) | data formatting | bytes 4489216
  97.7 1.4 %copy.15 = f32[548,8,128]{2,1,0:T(8,128)} copy(f32[548,8,128]{2,1,0:T(8,128)S(1)} %bitcast.8) | data formatting | bytes 4489216
Async XLA Ops:
  0.6 47.2 %copy-start.3 = (f32[548]{0:T(1024)S(1)}, f32[548]{0:T(1024)}, u32[]{:S(2)}) copy-start(f32[548]{0:T(1024)} %std_ref.1) | copy-start | bytes 6580
  0.6 47.2 %copy-start.5 = (f32[150]{0:T(256)S(1)}, f32[150]{0:T(256)}, u32[]{:S(2)}) copy-start(f32[150]{0:T(256)} %inv_ref.1) | copy-start | bytes 1804
  0.7 47.2 %copy-start.1 = (f32[96,150]{0,1:T(8,128)S(1)}, f32[96,150]{0,1:T(8,128)}, u32[]{:S(2)}) copy-start(f32[96,150]{0,1:T(8,128)} %param.12) | copy-start | bytes 172804
  0.7 47.2 %copy-start.4 = (s32[96,1]{0,1:T(1,128)S(1)}, s32[96,1]{0,1:T(1,128)}, u32[]{:S(2)}) copy-start(s32[96,1]{0,1:T(1,128)} %param.9) | copy-start | bytes 1156
  47.9 1.0 copy-start
  48.9 0.8 copy-start.2
  49.6 46.7 %copy-start.6 = (f32[4384,128]{1,0:T(8,128)S(1)}, f32[4384,128]{1,0:T(8,128)}, u32[]{:S(2)}) copy-start(f32[4384,128]{1,0:T(8,128)} %get-tuple-element.11) | copy-start | bytes 6733828

commit v7 on v6

--- a/solution.py
+++ b/solution.py
@@ -823,7 +823,6 @@
     swap(1, 0).start()
     receive_rest()
     send_lon(2, 0)
-    swap(2, 0).start()
     pass_on(0, 0)
     await_lon(0, 0)
     swap(0, 1).start()
@@ -831,23 +830,23 @@
     pass_on(1, 0)
     send_lon(1, 0)
     send_lon(1, 1)
-    pass_on(2, 0)
+    swap(2, 0).start()
     await_lon(2, 0)
     swap(2, 1).start()
     swap(2, 2).start()
     await_far(1, 0)
     send_lon(1, 2)
-    for j in lon_first:
-        pass_on(j, 1)
-        pass_on(j, 2)
-    for j in chunks:
-        if j in lon_first:
-            for b in range(3):
-                await_far(j, b)
-        else:
-            for a in range(3):
-                await_lon(j, a)
-        compute(j)
+    for j, b in ((0, 1), (0, 2), (2, 0), (2, 1), (2, 2)):
+        pass_on(j, b)
+    for b in range(3):
+        await_far(0, b)
+    compute(0)
+    for b in range(3):
+        await_far(2, b)
+    compute(2)
+    for a in range(3):
+        await_lon(1, a)
+    compute(1)
     for j in chunks:
         for b in range(3) if j in lon_first else (0,):
             swap(j, b).wait_send()

time: 100 us -> 99.2 us (level)
  no operation moved by 1% of the time
where the time goes in v7:
time: 99.2 us; the launch traced here: 98.1 us
  Pallas kernels  92.3 us (93%)
  local copies, waits for them, and re-layouts  5.11 us (5%)
    pallas_call x1, Pallas kernels, dense_step(): pl.pallas_call(functools.partial(dense_kernel, lat, lon, lat_rows, slots_...  47.2 us
    pallas_call x1, Pallas kernels, analysis_step(): pl.pallas_call(functools.partial(adjoint_kernel, lat, lon, lat_rows, slot...  45.1 us
    unnamed x17, local copies, waits for them, and re-layouts  5.11 us

profile of v7, /device:TPU:2, one launch (start us, length us, event | category | flops | bytes accessed | tf_op | source)
XLA Modules:
  0.0 98.1 jit_solution(13904678446916402535)
XLA Ops:
  0.6 0.0 copy-start.3
  0.6 0.0 copy-start.5
  0.7 0.0 copy-start.1
  0.7 0.0 copy-start.4
  0.7 47.2 %dense.1 = (f32[4384,128]{1,0:T(8,128)}, s32[32,1,256]{2,1,0:T(1,128)}, bf16[32,6,640]{2,1,0:T(8,128)(2,1)}) custom-call(f32[4384,128]{1,0:T(8,128)} %bitcast.14, s32[1,96]{1,0:T(1,128)} %bitcast.11, s32[1,96]{1,0:T(1,128)} %bitcast.16, f32[548]{0:T(1024)} %std_ref.1), custom_call_target="tpu_custom_call" | custom-call | tf_op jit(solution)/shard_map/dense/pallas_call | solution.py:497
  47.9 0.0 copy-done.3
  47.9 0.0 copy-done.5
  47.9 0.0 copy-done.1
  47.9 0.0 copy-done.4
  47.9 0.0 copy-start
  47.9 1.0 copy-done
  48.9 0.0 copy-start.2
  48.9 0.8 copy-done.2
  49.6 0.0 copy-start.6
  49.6 45.1 %analysis.1 = (f32[150,96]{1,0:T(8,128)S(1)}, f32[4384,128]{1,0:T(8,128)S(1)}) custom-call(bf16[150,96,548]{2,1,0:T(8,128)(2,1)} %bitcast.13, bf16[32,6,640]{2,1,0:T(8,128)(2,1)S(1)} %copy-done, s32[1,96]{1,0:T(1,128)S(1)} %bitcast.12, f32[150,96]{1,0:T(8,128)S(1)} %bitcast.9, f32[150]{0:T(256)S(1)} %copy-done.5, s32[32,1,256]{2,1,0:T(1,128)S(1)} %copy-done.2, ...), custom_call_target="tpu_custom_call" | custom-call | tf_op jit(solution)/shard_map/analysis/pallas_call | solution.py:874
  94.8 0.6 copy.13
  95.4 0.0 copy-done.6
  95.4 1.4 %copy.14 = f32[548,8,128]{2,1,0:T(8,128)} copy(f32[548,8,128]{2,1,0:T(8,128)S(1)} %bitcast.15) | data formatting | bytes 4489216
  96.8 1.4 %copy.15 = f32[548,8,128]{2,1,0:T(8,128)} copy(f32[548,8,128]{2,1,0:T(8,128)S(1)} %bitcast.8) | data formatting | bytes 4489216
Async XLA Ops:
  0.6 47.2 %copy-start.3 = (f32[548]{0:T(1024)S(1)}, f32[548]{0:T(1024)}, u32[]{:S(2)}) copy-start(f32[548]{0:T(1024)} %std_ref.1) | copy-start | bytes 6580
  0.6 47.2 %copy-start.5 = (f32[150]{0:T(256)S(1)}, f32[150]{0:T(256)}, u32[]{:S(2)}) copy-start(f32[150]{0:T(256)} %inv_ref.1) | copy-start | bytes 1804
  0.7 47.2 %copy-start.1 = (f32[96,150]{0,1:T(8,128)S(1)}, f32[96,150]{0,1:T(8,128)}, u32[]{:S(2)}) copy-start(f32[96,150]{0,1:T(8,128)} %param.12) | copy-start | bytes 172804
  0.7 47.2 %copy-start.4 = (s32[96,1]{0,1:T(1,128)S(1)}, s32[96,1]{0,1:T(1,128)}, u32[]{:S(2)}) copy-start(s32[96,1]{0,1:T(1,128)} %param.9) | copy-start | bytes 1156
  47.9 1.0 copy-start
  48.9 0.8 copy-start.2
  49.6 45.7 %copy-start.6 = (f32[4384,128]{1,0:T(8,128)S(1)}, f32[4384,128]{1,0:T(8,128)}, u32[]{:S(2)}) copy-start(f32[4384,128]{1,0:T(8,128)} %get-tuple-element.11) | copy-start | bytes 6733828
